TPU v7x, 32 devices: a whole 2x2x4 slice. The times are simulated.
32 devices in a mesh: gx: 4 (over y, core), gy: 2 (over x), gz: 4 (over z).
Axes of the slice: x: 2, y: 2, z: 4, core: 2. Of those that a mesh axis runs over, the one named last changes fastest.
Arguments:
- initial_hydraulic_head: float32 [1024, 128], P(('gx', 'gy', 'gz')), may hold values from -6 to 6
- well_discharge: float32 [1024, 128], P(('gx', 'gy', 'gz')), may hold values from -6 to 6
- local_facet_coupling: bfloat16 [1024, 128, 128], P(('gx', 'gy', 'gz')), may hold values from -0.25 to 0.25
- diagonal_capacity: float32 [1024, 128], P(('gx', 'gy', 'gz')), may hold values from 0.5 to 2
- crossing_permeability: float32 [1024, 4], P(('gx', 'gy', 'gz')), may hold values from 0.3 to 3
- crossing_partner_number: int32 [1024, 4], P(('gx', 'gy', 'gz')), may hold values from 0 to 255, as said below
- liquid_thermal_state: float32 [1024, 128], P(('gx', 'gy', 'gz')), may hold values from -6 to 6
- transfer_factor: float32 [1024, 128], P(('gx', 'gy', 'gz')), may hold values from 0.1 to 1
- host_voxel_number: int32 [1024, 128], P(('gx', 'gy', 'gz')), may hold values from 0 to 65535
- stone_thermal_state: float32 [64, 64, 512], P('gx', 'gy', 'gz'), may hold values from -6 to 6
- matrix_diffusivity: float32 [64, 64, 512], P('gx', 'gy', 'gz'), may hold values from 0.02 to 0.16
Outputs:
- updated_hydraulic_head: float32 [1024, 128], P(('gx', 'gy', 'gz'))
- diffused_thermal_state: float32 [64, 64, 512], P('gx', 'gy', 'gz')
Inputs may be any that keep to these rules, and one draw needn't show every extreme that they name: `crossing_partner_number`: coupling ids name blocks of devices with the same gz index: c // 32 is the index on gx+gy of the owning device and c % 32 the block on it. The 128 couplings of one device name the blocks of any one device of its group at most 32 times, and exactly 32 times for some device.
All inputs are finite; a program needn't handle non-finite values.
Results may differ from a plain program's by a relative error of at most 0.00053.
Values sent between devices are 32-bit elements; how exact they have to be, the bound alone decides.
No kernel may reach another device: no remote copies, remote signals or barrier semaphores. Data moves between devices by JAX's collectives and lax.ppermute only.
A program may use at most 64 MiB of HBM per device.

v0:
```python
import functools
import itertools

import jax
import jax.numpy as jnp
from jax import lax
from jax.experimental import pallas as pl
from jax.experimental.pallas import tpu as pltpu
from jax.sharding import PartitionSpec as P


SWEEPS = 3
AXES = ("gx", "gy", "gz")
GROUP = ("gx", "gy")
F32 = jnp.float32
BF16 = jnp.bfloat16
HIGH = lax.Precision.HIGHEST


def call(body, out_shape, *args, scratch=(), hbm=0):
    vmem = pl.BlockSpec(memory_space=pltpu.VMEM)
    args = [pltpu.with_memory_space_constraint(x, pltpu.HBM) for x in args[:hbm]] + list(args[hbm:])
    return pl.pallas_call(
        body,
        out_shape=out_shape,
        in_specs=[pl.BlockSpec(memory_space=pltpu.HBM)] * hbm + [vmem] * (len(args) - hbm),
        scratch_shapes=scratch,
        compiler_params=pltpu.CompilerParams(vmem_limit_bytes=48 << 20),
    )(*args)


def sds(shape, dtype=F32):
    return jax.ShapeDtypeStruct(shape, dtype)


def iota(shape, dim):
    return lax.broadcasted_iota(jnp.int32, shape, dim)


def dot(a, b, ca, cb, precision=None):
    return lax.dot_general(
        a, b, (((ca,), (cb,)), ((), ())), precision=precision, preferred_element_type=F32
    )


def group_size():
    return lax.axis_size("gx") * lax.axis_size("gy")


def by_pairs():
    return lax.axis_size("gx") == 4 and lax.axis_size("gy") == 2


def swap(x, k):
    n = group_size()
    return lax.ppermute(x, GROUP, [(i, i ^ k) for i in range(n)])


def meet(direct, own):
    low = lax.axis_size("gy")
    slots = {k: swap(x, k) for k, x in direct.items()}
    slots[low] = swap(own, low)
    for k in direct:
        slots[k | low] = swap(slots[k], low)
    return slots


def partner(axis, r, where):
    at, count, other = where[axis], lax.axis_size(axis), dict(where)
    up = at % 2 == r
    to = at + 1 if up else at - 1
    if 0 <= to < count:
        other[axis] = to
    elif axis == "gx":
        other[axis] = at if count % 2 else count - 1 - at
    elif lax.axis_size("gx") % 2 == 0:
        other["gx"] = where["gx"] ^ 1
    return other


def swap_list(axis, r):
    sizes = [lax.axis_size(a) for a in AXES]
    pairs = []
    for i, at in enumerate(itertools.product(*map(range, sizes))):
        other = partner(axis, r, dict(zip(AXES, at)))
        j = 0
        for a, size in zip(AXES, sizes):
            j = j * size + other[a]
        pairs.append((i, j))
    return pairs


def rounds_of(axis):
    count = lax.axis_size(axis)
    return 0 if count == 1 else 1 if count == 2 else 2


def face_specs(shape, lead):
    nx, ny, nz = shape
    full = {"gx": (lead, ny, nz), "gy": (lead, nx, nz), "gz": (lead, nx * ny)}
    return [(axis, r, full[axis]) for axis in AXES for r in range(rounds_of(axis))]


def exchange(faces, specs):
    out = []
    for face, (axis, r, _) in zip(faces, specs):
        out.append(lax.ppermute(face, AXES, swap_list(axis, r)))
    return out


def write_faces(refs, specs, fields):
    for j, t in enumerate(fields):
        nx, ny, nz = t.shape
        lanes = t.reshape(nx * ny, nz).T
        for ref, (axis, r, _) in zip(refs, specs):
            even = lax.axis_index(axis) % 2 == 0
            high = even if r == 0 else jnp.logical_not(even)
            if axis == "gx":
                ref[j] = jnp.where(high, t[nx - 1], t[0])
            elif axis == "gy":
                ref[j] = jnp.where(high, t[:, ny - 1, :], t[:, 0, :])
            else:
                ref[j : j + 1, :] = jnp.where(high, lanes[nz - 1 : nz], lanes[0:1])


def read_faces(refs, specs, j):
    got = {axis: [] for axis in AXES}
    for ref, (axis, r, _) in zip(refs, specs):
        got[axis].append(ref[j : j + 1, :] if axis == "gz" else ref[j])
    return got


def ghosts_of(axis, faces, like):
    zero = jnp.zeros(like, F32)
    if not faces:
        return zero, zero
    index, count = lax.axis_index(axis), lax.axis_size(axis)
    even = index % 2 == 0
    second = faces[1] if len(faces) > 1 else zero
    low = jnp.where(even, second, faces[0])
    high = jnp.where(even, faces[0], second)
    return jnp.where(index > 0, low, zero), jnp.where(index < count - 1, high, zero)


def embed_z(pair, shape):
    nx, ny, nz = shape
    low, high = pair
    return jnp.concatenate([low, jnp.zeros((nz - 2, nx * ny), F32), high], axis=0).T.reshape(shape)


def interior(t, c):
    shape = t.shape
    _, ny, nz = shape
    gain = jnp.zeros(shape, F32)
    weight = jnp.zeros(shape, F32)
    wx = 0.5 * (c[:-1] + c[1:])
    none = jnp.zeros((1, ny, nz), F32)
    w_low = jnp.concatenate([none, wx], axis=0)
    w_high = jnp.concatenate([wx, none], axis=0)
    t_low = jnp.concatenate([none, t[:-1]], axis=0)
    t_high = jnp.concatenate([t[1:], none], axis=0)
    gain = gain + w_low * t_low + w_high * t_high
    weight = weight + w_low + w_high
    for dim, n in ((1, ny), (2, nz)):
        at = iota(shape, dim)
        for shift, edge in ((1, 0), (n - 1, n - 1)):
            w = jnp.where(at == edge, 0.0, 0.5 * (c + pltpu.roll(c, shift, dim)))
            gain = gain + w * pltpu.roll(t, shift, dim)
            weight = weight + w
    return gain, weight


def shards(
    initial_hydraulic_head,
    well_discharge,
    local_facet_coupling,
    diagonal_capacity,
    crossing_permeability,
    crossing_partner_number,
    liquid_thermal_state,
    transfer_factor,
    host_voxel_number,
    stone_thermal_state,
    matrix_diffusivity,
):
    nb, links = crossing_partner_number.shape
    tri = initial_hydraulic_head.shape[1]
    shape = stone_thermal_state.shape
    nx, ny, nz = shape
    rows_n = nx * ny
    n = group_size()
    low = lax.axis_size("gy")
    pairs = by_pairs() and 4 * nb == tri
    specs2 = face_specs(shape, 2)
    specs1 = face_specs(shape, 1)
    xy = [i for i, spec in enumerate(specs2) if spec[0] != "gz"]
    zs = [i for i, spec in enumerate(specs2) if spec[0] == "gz"]
    blk = sds((nb, tri))
    slab = sds(shape)
    small = -(-2 * links // 8) * 8
    group = 8
    chunks = nb // group

    def load(copies):
        copies = [pltpu.make_async_copy(src, dst, sem) for src, dst, sem in copies]
        for copy in copies:
            copy.start()
        return copies

    def inner_of(a_ref, h, ready=None):
        h = h.astype(BF16)
        rows = []
        for b in range(0, nb, group):
            if ready:
                ready(b // group)
            both = dot(h[b : b + group, :], a_ref[b : b + group].reshape(group * tri, tri), 1, 1)
            rows += [both[i : i + 1, i * tri : (i + 1) * tri] for i in range(group)]
        return jnp.concatenate(rows, axis=0)

    def mix_of(ids, perm):
        at = iota((n * nb, ids.shape[1]), 0)
        mix = jnp.zeros(at.shape, F32)
        for k in range(links):
            mix = mix + jnp.where(at == ids[k : k + 1, :], perm[k : k + 1, :], 0.0)
        return mix

    def pre(*refs):
        hbm, (send_ref, w_ref, *rock, a_ref), (ids_ref, perm_ref, den_ref, h_ref, sems) = refs[:11], refs[11:19], refs[19:]
        a_hbm = hbm[5]
        pieces = list(zip(hbm[:5], (ids_ref, perm_ref, den_ref, h_ref, w_ref)))
        for i in range(chunks):
            part = pl.ds(i * group, group)
            pieces.append((a_hbm.at[part], a_ref.at[part]))
        pieces += list(zip(hbm[6:], rock))
        copies = load([(src, dst, sems.at[i]) for i, (src, dst) in enumerate(pieces)])
        send_ref[3 * nb :, :] = jnp.zeros((small, tri), F32)
        for copy in copies[:5]:
            copy.wait()
        perm = perm_ref[...]
        send_ref[3 * nb : 3 * nb + links, :nb] = ids_ref[...].astype(F32)
        send_ref[3 * nb + links : 3 * nb + 2 * links, :nb] = perm
        rows = jnp.concatenate([perm, jnp.zeros((-links % 8, nb), F32)], axis=0)
        send_ref[2 * nb : 3 * nb, :] = den_ref[...] + dot(rows, jnp.ones((rows.shape[0], tri), F32), 0, 0, HIGH)
        h = h_ref[...]
        send_ref[:nb, :] = h
        send_ref[nb : 2 * nb, :] = w_ref[...] + inner_of(a_ref, h, lambda i: copies[5 + i].wait())
        for copy in copies[5 + chunks :]:
            copy.wait()

    def rock(t_ref, c_ref, *faces):
        write_faces(faces, specs2, (t_ref[...], c_ref[...]))

    def both(w_ref, a_ref, *rest):
        slots, rest = rest[:n], rest[n:]
        faces, (h_ref, mix_ref, *sends) = rest[: len(xy)], rest[len(xy) :]
        me = lax.axis_index("gx") * low + lax.axis_index("gy")
        heads = jnp.concatenate([s[:nb, :] for s in slots], axis=0)
        per = tri // nb
        first = []
        for g in range(0, n, per):
            table = slots[g][3 * nb :, :]
            for i in range(1, per):
                table = table + pltpu.roll(slots[g + i][3 * nb :, :], i * nb, 1)
            ids = table[:links, :].astype(jnp.int32) ^ (me * nb)
            mix = mix_of(ids, table[links : 2 * links, :])
            if g == 0:
                mix_ref[...] = mix
            across = dot(mix, heads, 0, 0, HIGH)
            for i in range(per):
                s = slots[g + i]
                first.append((s[nb : 2 * nb, :] + across[i * nb : (i + 1) * nb, :]) / s[2 * nb : 3 * nb, :])
        inner = inner_of(a_ref, first[0])
        across = dot(mix_ref[...], jnp.concatenate(first, axis=0), 0, 0, HIGH)[:nb, :]
        h = (w_ref[...] + inner + across) / slots[0][2 * nb : 3 * nb, :]
        h_ref[...] = h
        for send, face in zip(sends, faces):
            send[:nb, :] = h
            half = face.shape[1]
            send[nb : nb + half, :] = face[0]
            send[nb + half : nb + 2 * half, :] = face[1]

    def inner_body(a_ref, h_ref, o_ref):
        o_ref[...] = inner_of(a_ref, h_ref[...])

    def sweep(w_ref, den_ref, mix_ref, inner_ref, heads):
        across = dot(mix_ref[...], heads, 0, 0, HIGH)[:nb, :]
        return (w_ref[...] + inner_ref[...] + across) / den_ref[...]

    def gather(first, t_ref, hv_ref, liq_ref, tf_ref, q_ref, hot_ref):
        t = t_ref[...].reshape(rows_n, nz)
        hi = t.astype(BF16)
        lo = (t - hi.astype(F32)).astype(BF16)
        parts = jnp.concatenate([hi, lo], axis=1)
        hv = hv_ref[...]
        step = 4
        half = hot_ref.shape[1] // tri
        for b in range(0, half, step):
            cell = jnp.concatenate([hv[first + i : first + i + 1, :] for i in range(b, b + step)], axis=1)
            width = step * tri
            mine = lax.broadcasted_iota(jnp.int16, (rows_n, width), 0) == (cell // nz).astype(jnp.int16)
            hot = jnp.where(mine, jnp.ones((), BF16), jnp.zeros((), BF16))
            hot_ref[:, b * tri : b * tri + width] = hot
            rows = dot(parts, hot, 0, 0)
            rows = rows[:nz] + rows[nz:]
            value = jnp.sum(jnp.where(iota((nz, width), 0) == cell % nz, rows, 0.0), axis=0, keepdims=True)
            for i in range(step):
                q_ref[b + i : b + i + 1, :] = value[:, i * tri : (i + 1) * tri]
        own = slice(first, first + half)
        q_ref[...] = tf_ref[own, :] * (liq_ref[own, :] - q_ref[...])

    def base(t_ref, c_ref, *rest):
        got, (u_ref, keep_ref, wz_ref) = rest[: len(zs)], rest[len(zs) :]
        specs = [specs2[i] for i in zs]
        t, c = t_ref[...], c_ref[...]
        tz = ghosts_of("gz", read_faces(got, specs, 0)["gz"], (1, rows_n))
        cz = ghosts_of("gz", read_faces(got, specs, 1)["gz"], (1, rows_n))
        gain, weight = interior(t, c)
        at = iota(shape, 2)
        wz = jnp.where((at == 0) | (at == nz - 1), 0.5 * (c + embed_z(cz, shape)), 0.0)
        keep = 1.0 - weight - wz
        wz_ref[...] = wz
        keep_ref[...] = keep
        u_ref[...] = gain + t * keep + wz * embed_z(tz, shape)

    def add_sides(u_ref, t_ref, wx_ref, wy_ref, gx, gy):
        for i, at in enumerate((0, nx - 1)):
            u_ref[at] = u_ref[at] + wx_ref[i] * (gx[i] - t_ref[at])
        for i, at in enumerate((0, ny - 1)):
            u_ref[:, at, :] = u_ref[:, at, :] + wy_ref[i] * (gy[i] - t_ref[:, at, :])

    def heat(get_sides, get_heads, ns, *refs):
        mix_ref, den_ref, w_ref, inner_ref, q1_ref, q2_ref, hv_ref, hot1_ref, hot2_ref, u_ref, t0_ref, c_ref = refs[:12]
        got, rest = refs[12 : 12 + ns], refs[12 + ns :]
        h_ref, f_ref, t_ref, wx_ref, wy_ref, *faces = rest[:-1]
        pick_ref = rest[-1]
        h = sweep(w_ref, den_ref, mix_ref, inner_ref, get_heads(got))
        h_ref[...] = h
        q = jnp.concatenate([q1_ref[...], q2_ref[...]], axis=0)
        flux = q * jnp.sqrt(1.0 + h * h)
        hi = flux.astype(BF16)
        lo = (flux - hi.astype(F32)).astype(BF16)
        lane = (hv_ref[...] % nz).astype(jnp.int16)
        at = lax.broadcasted_iota(jnp.int16, (nz, tri), 0)
        none = jnp.zeros((), BF16)
        for b in range(nb):
            mine = at == lane[b : b + 1, :]
            pick_ref[:nz, b * tri : (b + 1) * tri] = jnp.where(mine, hi[b : b + 1, :], none)
            pick_ref[nz:, b * tri : (b + 1) * tri] = jnp.where(mine, lo[b : b + 1, :], none)
        half = hot1_ref.shape[1]
        parts = dot(hot1_ref[...], pick_ref[:, :half], 1, 1) + dot(hot2_ref[...], pick_ref[:, half:], 1, 1)
        f = (parts[:, :nz] + parts[:, nz:]).reshape(shape)
        f_ref[...] = f
        t_ref[...] = u_ref[...] + f
        tx, ty = get_sides(got, 0)
        cx, cy = get_sides(got, 1)
        for i, at in enumerate((0, nx - 1)):
            wx_ref[i] = 0.5 * (c_ref[at] + cx[i])
        for i, at in enumerate((0, ny - 1)):
            wy_ref[i] = 0.5 * (c_ref[:, at, :] + cy[i])
        add_sides(t_ref, t0_ref, wx_ref, wy_ref, tx, ty)
        write_faces(faces, specs1, (t_ref[...],))

    def middle(t_ref, f_ref, c_ref, keep_ref, v_ref):
        t = t_ref[...]
        gain, _ = interior(t, c_ref[...])
        v_ref[...] = f_ref[...] + t * keep_ref[...] + gain

    def last(h_ref, v_ref, t_ref, wx_ref, wy_ref, wz_ref, *rest):
        got, (head_ref, o_ref) = rest[:-2], rest[-2:]
        head_ref[...] = h_ref[...]
        faces = read_faces(got, specs1, 0)
        o_ref[...] = v_ref[...] + wz_ref[...] * embed_z(ghosts_of("gz", faces["gz"], (1, rows_n)), shape)
        gx = ghosts_of("gx", faces["gx"], (ny, nz))
        gy = ghosts_of("gy", faces["gy"], (nx, nz))
        add_sides(o_ref, t_ref, wx_ref, wy_ref, gx, gy)

    send, w, t, c, hv, liq, tf, a = call(
        pre,
        [sds((3 * nb + small, tri)), blk, slab, slab, sds((nb, tri), jnp.int32), blk, blk]
        + [sds(local_facet_coupling.shape, BF16)],
        crossing_partner_number.T,
        crossing_permeability.T,
        diagonal_capacity,
        initial_hydraulic_head,
        well_discharge,
        local_facet_coupling,
        stone_thermal_state,
        matrix_diffusivity,
        host_voxel_number,
        liquid_thermal_state,
        transfer_factor,
        scratch=[pltpu.VMEM((links, nb), jnp.int32), pltpu.VMEM((links, nb), F32)]
        + [pltpu.VMEM((nb, tri), F32)] * 2
        + [pltpu.SemaphoreType.DMA((10 + chunks,))],
        hbm=11,
    )
    if pairs:
        slots = meet({k: send for k in range(n - 1, 0, -1) if not k & low}, send)
    faces = call(rock, [sds(s) for _, _, s in specs2], t, c)
    got_z = exchange([faces[i] for i in zs], [specs2[i] for i in zs])
    if pairs:
        y_at, xa_at, xb_at = 1, low, 2 * low
        order = {"gx": (xa_at, xb_at), "gy": (y_at,)}
        rides = [order[specs2[i][0]][specs2[i][1]] for i in xy]
        h, mix, *sends = call(
            both,
            [blk, sds((n * nb, tri))] + [sds((nb + 2 * specs2[i][2][1], tri)) for i in xy],
            w,
            a,
            send,
            *[slots[k] for k in range(1, n)],
            *[faces[i] for i in xy],
        )
        ride = dict(zip(rides, sends))
        slots = meet({k: ride.get(k, h) for k in range(n - 1, 0, -1) if not k & low}, ride[low])
        den = send[2 * nb : 3 * nb]
        got = [h] + [slots[k] for k in range(1, n)]

        def get_heads(refs):
            return jnp.concatenate([r[:nb, :] for r in refs], axis=0)

        def get_sides(refs, j):
            x_rows, y_rows = slice(nb + j * ny, nb + (j + 1) * ny), slice(nb + j * nx, nb + (j + 1) * nx)
            gx = ghosts_of("gx", [refs[xa_at][x_rows, :], refs[xb_at | low][x_rows, :]], (ny, nz))
            return gx, ghosts_of("gy", [refs[y_at][y_rows, :]], (nx, nz))
    else:
        den = send[2 * nb : 3 * nb]
        h = initial_hydraulic_head
        ids = jnp.zeros((small, tri), jnp.int32).at[:links, :nb].set(crossing_partner_number.T)
        perm = send[3 * nb + links : 3 * nb + 2 * links]

        def mix_body(ids_ref, perm_ref, mix_ref):
            mix_ref[...] = mix_of(ids_ref[...], perm_ref[...])

        def sweep_body(w_ref, den_ref, mix_ref, inner_ref, heads_ref, h_ref):
            h_ref[...] = sweep(w_ref, den_ref, mix_ref, inner_ref, heads_ref[...])

        mix = call(mix_body, sds((n * nb, tri)), ids[:links], perm)
        for _ in range(SWEEPS - 1):
            heads = lax.all_gather(h, GROUP, axis=0, tiled=True)
            inner = call(inner_body, blk, a, h)
            h = call(sweep_body, blk, w, den, mix, inner, heads)
        got = [lax.all_gather(h, GROUP, axis=0, tiled=True)]
        got += exchange([faces[i] for i in xy], [specs2[i] for i in xy])

        def get_heads(refs):
            return refs[0][...]

        def get_sides(refs, j):
            sides = read_faces(refs[1:], [specs2[i] for i in xy], j)
            return ghosts_of("gx", sides["gx"], (ny, nz)), ghosts_of("gy", sides["gy"], (nx, nz))

    inner = call(inner_body, blk, a, h)
    half = nb // 2
    parts = [
        call(functools.partial(gather, i * half), (sds((half, tri)), sds((rows_n, half * tri), BF16)), t, hv, liq, tf)
        for i in range(2)
    ]
    (q1, hot1), (q2, hot2) = parts
    u, keep, wz = call(base, (slab, slab, slab), t, c, *got_z)
    h, f, t1, wx, wy, *faces = call(
        functools.partial(heat, get_sides, get_heads, len(got)),
        [blk, slab, slab, sds((2, ny, nz)), sds((2, nx, nz))] + [sds(s) for _, _, s in specs1],
        mix,
        den,
        w,
        inner,
        q1,
        q2,
        hv,
        hot1,
        hot2,
        u,
        t,
        c,
        *got,
        scratch=[pltpu.VMEM((2 * nz, nb * tri), BF16)],
    )
    got = exchange(faces, specs1)
    v = call(middle, slab, t1, f, c, keep)
    h, out = call(last, (blk, slab), h, v, t1, wx, wy, wz, *got)
    return (h, out)


def solution(mesh):
    block = P(AXES, None)
    rock = P(*AXES)
    in_specs = (block, block, P(AXES, None, None)) + (block,) * 6 + (rock, rock)

    return jax.shard_map(shards, mesh=mesh, in_specs=in_specs, out_specs=(block, rock), check_vma=False)
```

profile of v0, /device:TPU:0, one launch (start us, length us, event | category | flops | bytes accessed | tf_op | source)
XLA Modules:
  0.0 38.5 jit_solution(15170156799513749978)
XLA Ops:
  0.6 1.9 %shard_map.122 = (f32[104,128]{1,0:T(8,128)S(1)}, f32[32,128]{1,0:T(8,128)S(1)}, f32[16,32,128]{2,1,0:T(8,128)S(1)}, f32[16,32,128]{2,1,0:T(8,128)S(1)}, s32[32,...) custom-call(s32[4,32]{1,0:T(4,128)} %bitcast.2, ...), custom_call_target="tpu_custom_call" | custom-call | tf_op jit(solution)/shard_map/pallas_call | solution.py:23
  2.6 4.0 %collective-permute-start.4 = (f32[104,128]{1,0:T(8,128)S(1)}, f32[104,128]{1,0:T(8,128)S(1)}, u32[]{:S(2)}, u32[]{:S(2)}) collective-permute-start(f32[104,128]{1,0:T(8,128)S(1)} %get-tuple-element.39.rest_0_), channel_id=1, source_target_pairs={{0,20},{4,16},{8,28},{12,24},{16,4},{20,0},{24,12},{28,8},{1,21},{... | collective-permute-start | bytes 159752 | tf_op jit(solution)/shard_map/ppermute | solution.py:56
  6.5 0.5 %collective-permute-start.3 = (f32[104,128]{1,0:T(8,128)S(1)}, f32[104,128]{1,0:T(8,128)S(1)}, u32[]{:S(2)}, u32[]{:S(2)}) collective-permute-start(f32[104,128]{1,0:T(8,128)S(1)} %get-tuple-element.39.rest_0_), channel_id=1, source_target_pairs={{0,16},{4,20},{8,24},{12,28},{16,0},{20,4},{24,8},{28,12},{1,17},{... | collective-permute-start | bytes 159752 | tf_op jit(solution)/shard_map/ppermute | solution.py:56
  7.0 0.1 collective-permute-start
  7.2 0.0 collective-permute-start.1
  7.2 1.5 %collective-permute-done.4.rest_5_ = f32[104,128]{1,0:T(8,128)S(1)} collective-permute-done((f32[104,128]{1,0:T(8,128)S(1)}, f32[104,128]{1,0:T(8,128)S(1)}, u32[]{:S(2)}, u32[]{:S(2)}) %collective-permute-start.4) | collective-permute-done | bytes 53280 | tf_op jit(solution)/shard_map/ppermute | solution.py:56
  8.7 0.0 collective-permute-start.6
  8.7 2.0 %collective-permute-done.3.rest_4_ = f32[104,128]{1,0:T(8,128)S(1)} collective-permute-done((f32[104,128]{1,0:T(8,128)S(1)}, f32[104,128]{1,0:T(8,128)S(1)}, u32[]{:S(2)}, u32[]{:S(2)}) %collective-permute-start.3) | collective-permute-done | bytes 53280 | tf_op jit(solution)/shard_map/ppermute | solution.py:56
  10.7 0.0 collective-permute-start.5
  10.7 0.5 %collective-permute-done.rest_1_ = f32[104,128]{1,0:T(8,128)S(1)} collective-permute-done((f32[104,128]{1,0:T(8,128)S(1)}, f32[104,128]{1,0:T(8,128)S(1)}, u32[]{:S(2)}, u32[]{:S(2)}) %collective-permute-start) | collective-permute-done | bytes 53280 | tf_op jit(solution)/shard_map/ppermute | solution.py:56
  11.2 0.0 collective-permute-start.2
  11.2 0.2 shard_map.123
  11.4 0.0 collective-permute-done.1.rest_2_
  11.4 0.0 collective-permute-done.6.rest_7_
  11.4 0.5 %collective-permute-done.5.rest_6_ = f32[104,128]{1,0:T(8,128)S(1)} collective-permute-done((f32[104,128]{1,0:T(8,128)S(1)}, f32[104,128]{1,0:T(8,128)S(1)}, u32[]{:S(2)}, u32[]{:S(2)}) %collective-permute-start.5) | collective-permute-done | bytes 53280 | tf_op jit(solution)/shard_map/ppermute | solution.py:56
  11.9 0.5 %collective-permute-done.2.rest_3_ = f32[104,128]{1,0:T(8,128)S(1)} collective-permute-done((f32[104,128]{1,0:T(8,128)S(1)}, f32[104,128]{1,0:T(8,128)S(1)}, u32[]{:S(2)}, u32[]{:S(2)}) %collective-permute-start.2) | collective-permute-done | bytes 53280 | tf_op jit(solution)/shard_map/ppermute | solution.py:56
  12.4 1.0 %shard_map.124 = (f32[32,128]{1,0:T(8,128)S(1)}, f32[256,128]{1,0:T(8,128)S(1)}, f32[96,128]{1,0:T(8,128)S(1)}, f32[96,128]{1,0:T(8,128)S(1)}, f32[64,128]{1,0:T(8,128)S(1)}) custom-call(f32[32,128]{1,0:T(8,128)S(1)} %get-tuple-element.37.w_ref.refs_2_, bf16[32,128,128]{2,1,0:T(8,128)(2,1)S(1)} %get-tuple-element.38.a_ref, ...), custom_call_target="tpu_custom_call" | custom-call | tf_op jit(solution)/shard_map/pallas_call | solution.py:23
  13.4 1.6 %collective-permute-start.12 = (f32[96,128]{1,0:T(8,128)S(1)}, f32[96,128]{1,0:T(8,128)S(1)}, u32[]{:S(2)}, u32[]{:S(2)}) collective-permute-start(f32[96,128]{1,0:T(8,128)S(1)} %get-tuple-element.59), channel_id=1, source_target_pairs={{0,16},{4,20},{8,24},{12,28},{16,0},{20,4},{24,8},{28,12},{1,17},{... | collective-permute-start | bytes 147464 | tf_op jit(solution)/shard_map/ppermute | solution.py:56
  15.0 0.5 %collective-permute-start.9 = (f32[64,128]{1,0:T(8,128)S(1)}, f32[64,128]{1,0:T(8,128)S(1)}, u32[]{:S(2)}, u32[]{:S(2)}) collective-permute-start(f32[64,128]{1,0:T(8,128)S(1)} %get-tuple-element.57), channel_id=1, source_target_pairs={{0,4},{4,0},{8,12},{12,8},{16,20},{20,16},{24,28},{28,24},{1,5},{5... | collective-permute-start | bytes 98312 | tf_op jit(solution)/shard_map/ppermute | solution.py:56
  15.5 0.0 collective-permute-start.10
  15.5 2.0 %collective-permute-done.12.refs_16_ = f32[96,128]{1,0:T(8,128)S(1)} collective-permute-done((f32[96,128]{1,0:T(8,128)S(1)}, f32[96,128]{1,0:T(8,128)S(1)}, u32[]{:S(2)}, u32[]{:S(2)}) %collective-permute-start.12) | collective-permute-done | bytes 49184 | tf_op jit(solution)/shard_map/ppermute | solution.py:56
  17.5 0.0 collective-permute-start.14
  17.5 1.5 %collective-permute-start.13 = (f32[32,128]{1,0:T(8,128)S(1)}, f32[32,128]{1,0:T(8,128)S(1)}, u32[]{:S(2)}, u32[]{:S(2)}) collective-permute-start(f32[32,128]{1,0:T(8,128)S(1)} %get-tuple-element.46.h_ref.refs_12_), channel_id=1, source_target_pairs={{0,20},{4,16},{8,28},{12,24},{16,4},{20,0},{24,12},{28,8},{1,21},{... | collective-permute-start | bytes 49160 | tf_op jit(solution)/shard_map/ppermute | solution.py:56
  19.0 0.0 collective-permute-done.9.refs_13_
  19.0 0.2 collective-permute-start.11
  19.3 2.9 %collective-permute-done.13.refs_17_ = f32[32,128]{1,0:T(8,128)S(1)} collective-permute-done((f32[32,128]{1,0:T(8,128)S(1)}, f32[32,128]{1,0:T(8,128)S(1)}, u32[]{:S(2)}, u32[]{:S(2)}) %collective-permute-start.13) | collective-permute-done | bytes 16416 | tf_op jit(solution)/shard_map/ppermute | solution.py:56
  22.2 0.0 collective-permute-start.15
  22.2 1.6 %collective-permute-start.7 = (f32[2,512]{1,0:T(2,128)S(1)}, f32[2,512]{1,0:T(2,128)S(1)}, u32[]{:S(2)}, u32[]{:S(2)}) collective-permute-start(f32[2,512]{1,0:T(2,128)S(1)} %get-tuple-element.54), channel_id=1, source_target_pairs={{0,1},{1,0},{2,3},{3,2},{4,5},{5,4},{6,7},{7,6},{8,9},{9,8},{10,11... | collective-permute-start | bytes 12296 | tf_op jit(solution)/shard_map/ppermute | solution.py:107
  23.8 2.0 %collective-permute-done.7.rest_0_ = f32[2,512]{1,0:T(2,128)S(1)} collective-permute-done((f32[2,512]{1,0:T(2,128)S(1)}, f32[2,512]{1,0:T(2,128)S(1)}, u32[]{:S(2)}, u32[]{:S(2)}) %collective-permute-start.7) | collective-permute-done | bytes 4128 | tf_op jit(solution)/shard_map/ppermute | solution.py:107
  25.8 0.0 collective-permute-start.8
  25.8 0.8 %shard_map.127 = (f32[16,128]{1,0:T(8,128)S(1)}, bf16[512,2048]{1,0:T(8,128)(2,1)S(1)}) custom-call(f32[16,32,128]{2,1,0:T(8,128)S(1)} %get-tuple-element.40.t_ref.refs_10_, s32[32,128]{1,0:T(8,128)S(1)} %get-tuple-element.47.hv_ref.refs_6_, f32[32,128]{1,0:T(8,128)S(1)} %get-tuple-element.48.liq_ref, f32[32,128]{1,0:T(8,128)S(1)} %get-tuple-element.49.tf_ref), custom_call_target="tpu_custom_call" | custom-call | tf_op jit(solution)/shard_map/pallas_call | solution.py:23
  26.6 0.8 %shard_map.126 = (f32[16,128]{1,0:T(8,128)S(1)}, bf16[512,2048]{1,0:T(8,128)(2,1)S(1)}) custom-call(f32[16,32,128]{2,1,0:T(8,128)S(1)} %get-tuple-element.40.t_ref.refs_10_, s32[32,128]{1,0:T(8,128)S(1)} %get-tuple-element.47.hv_ref.refs_6_, f32[32,128]{1,0:T(8,128)S(1)} %get-tuple-element.48.liq_ref, f32[32,128]{1,0:T(8,128)S(1)} %get-tuple-element.49.tf_ref), custom_call_target="tpu_custom_call" | custom-call | tf_op jit(solution)/shard_map/pallas_call | solution.py:23
  27.4 0.0 collective-permute-done.8.rest_1_
  27.4 0.6 %shard_map.128 = (f32[16,32,128]{2,1,0:T(8,128)S(1)}, f32[16,32,128]{2,1,0:T(8,128)S(1)}, f32[16,32,128]{2,1,0:T(8,128)S(1)}) custom-call(f32[16,32,128]{2,1,0:T(8,128)S(1)} %get-tuple-element.40.t_ref.refs_10_, f32[16,32,128]{2,1,0:T(8,128)S(1)} %get-tuple-element.41.c_ref.refs_11_, f32[2,512]{1,0:T(2,128)S(1)} %collective-permute-done.7.rest_0_, ...), custom_call_target="tpu_custom_call" | custom-call | tf_op jit(solution)/shard_map/pallas_call | solution.py:23
  28.0 0.4 shard_map.125.refs_3_
  28.4 0.0 collective-permute-done.15.refs_19_
  28.4 0.0 collective-permute-done.10.refs_14_
  28.4 0.0 collective-permute-done.11.refs_15_
  28.4 0.0 collective-permute-done.14.refs_18_
  28.4 1.8 %shard_map.129 = (f32[32,128]{1,0:T(8,128)S(1)}, f32[16,32,128]{2,1,0:T(8,128)S(1)}, f32[16,32,128]{2,1,0:T(8,128)S(1)}, f32[2,32,128]{2,1,0:T(8,128)S(1)}, f32[...) custom-call(f32[256,128]{1,0:T(8,128)S(1)} %get-tuple-element.45.ref, ...), custom_call_target="tpu_custom_call" | custom-call | tf_op jit(solution)/shard_map/pallas_call | solution.py:23
  30.2 0.6 %collective-permute-start.16 = (f32[1,32,128]{2,1,0:T(8,128)S(1)}, f32[1,32,128]{2,1,0:T(8,128)S(1)}, u32[]{:S(2)}, u32[]{:S(2)}) collective-permute-start(f32[1,32,128]{2,1,0:T(8,128)S(1)} %get-tuple-element.67), channel_id=1, source_target_pairs={{0,8},{1,9},{2,10},{3,11},{4,12},{5,13},{6,14},{7,15},{8,0},{9,1},... | collective-permute-start | bytes 49160 | tf_op jit(solution)/shard_map/ppermute | solution.py:107
  30.8 1.2 %collective-permute-start.17 = (f32[1,32,128]{2,1,0:T(8,128)S(1)}, f32[1,32,128]{2,1,0:T(8,128)S(1)}, u32[]{:S(2)}, u32[]{:S(2)}) collective-permute-start(f32[1,32,128]{2,1,0:T(8,128)S(1)} %get-tuple-element.68), channel_id=1, source_target_pairs={{0,24},{1,25},{2,26},{3,27},{4,28},{5,29},{6,30},{7,31},{8,16},{9,... | collective-permute-start | bytes 49160 | tf_op jit(solution)/shard_map/ppermute | solution.py:107
  32.0 0.5 %collective-permute-start.18 = (f32[1,16,128]{2,1,0:T(8,128)S(1)}, f32[1,16,128]{2,1,0:T(8,128)S(1)}, u32[]{:S(2)}, u32[]{:S(2)}) collective-permute-start(f32[1,16,128]{2,1,0:T(8,128)S(1)} %get-tuple-element.69), channel_id=1, source_target_pairs={{0,4},{1,5},{2,6},{3,7},{4,0},{5,1},{6,2},{7,3},{8,12},{9,13},{10,... | collective-permute-start | bytes 24584 | tf_op jit(solution)/shard_map/ppermute | solution.py:107
  32.5 3.5 %collective-permute-start.19 = (f32[1,512]{1,0:T(1,128)S(1)}, f32[1,512]{1,0:T(1,128)S(1)}, u32[]{:S(2)}, u32[]{:S(2)}) collective-permute-start(f32[1,512]{1,0:T(1,128)S(1)} %get-tuple-element.70), channel_id=1, source_target_pairs={{0,1},{1,0},{2,3},{3,2},{4,5},{5,4},{6,7},{7,6},{8,9},{9,8},{10,11... | collective-permute-start | bytes 6152 | tf_op jit(solution)/shard_map/ppermute | solution.py:107
  36.0 0.0 collective-permute-start.20
  36.0 0.4 %shard_map.130.v_ref = f32[16,32,128]{2,1,0:T(8,128)S(1)} custom-call(f32[16,32,128]{2,1,0:T(8,128)S(1)} %get-tuple-element.61.t_ref, f32[16,32,128]{2,1,0:T(8,128)S(1)} %get-tuple-element.62.f_ref, f32[16,32,128]{2,1,0:T(8,128)S(1)} %get-tuple-element.41.c_ref.refs_11_, f32[16,32,128]{2,1,0:T(8,128)S(1)} %get-tuple-element.63.keep_ref), custom_call_target="tpu_custom_call" | custom-call | tf_op jit(solution)/shard_map/pallas_call | solution.py:23
  36.4 1.2 %collective-permute-done.19.rest_3_ = f32[1,512]{1,0:T(1,128)S(1)} collective-permute-done((f32[1,512]{1,0:T(1,128)S(1)}, f32[1,512]{1,0:T(1,128)S(1)}, u32[]{:S(2)}, u32[]{:S(2)}) %collective-permute-start.19) | collective-permute-done | bytes 2080 | tf_op jit(solution)/shard_map/ppermute | solution.py:107
  37.6 0.0 collective-permute-done.20.rest_4_
  37.6 0.0 collective-permute-done.18.rest_2_
  37.6 0.0 collective-permute-done.16.rest_0_
  37.6 0.0 collective-permute-done.17.rest_1_
  37.6 0.9 %shard_map.131 = (f32[32,128]{1,0:T(8,128)}, f32[16,32,128]{2,1,0:T(8,128)}) custom-call(f32[32,128]{1,0:T(8,128)S(1)} %get-tuple-element.60.h_ref, f32[16,32,128]{2,1,0:T(8,128)S(1)} %shard_map.130.v_ref, f32[16,32,128]{2,1,0:T(8,128)S(1)} %get-tuple-element.61.t_ref, f32[2,32,128]{2,1,0:T(8,128)S(1)} %get-tuple-element.64.wx_ref, ...), custom_call_target="tpu_custom_call" | custom-call | tf_op jit(solution)/shard_map/pallas_call | solution.py:23
  (1 shorter events, 0.0 us)
Async XLA Ops:
  2.6 6.1 %collective-permute-start.4 = (f32[104,128]{1,0:T(8,128)S(1)}, f32[104,128]{1,0:T(8,128)S(1)}, u32[]{:S(2)}, u32[]{:S(2)}) collective-permute-start(f32[104,128]{1,0:T(8,128)S(1)} %get-tuple-element.39.rest_0_), channel_id=1, source_target_pairs={{0,20},{4,16},{8,28},{12,24},{16,4},{20,0},{24,12},{28,8},{1,21},{... | collective-permute-start | bytes 159752 | tf_op jit(solution)/shard_map/ppermute | solution.py:56
  6.5 4.1 %collective-permute-start.3 = (f32[104,128]{1,0:T(8,128)S(1)}, f32[104,128]{1,0:T(8,128)S(1)}, u32[]{:S(2)}, u32[]{:S(2)}) collective-permute-start(f32[104,128]{1,0:T(8,128)S(1)} %get-tuple-element.39.rest_0_), channel_id=1, source_target_pairs={{0,16},{4,20},{8,24},{12,28},{16,0},{20,4},{24,8},{28,12},{1,17},{... | collective-permute-start | bytes 159752 | tf_op jit(solution)/shard_map/ppermute | solution.py:56
  7.0 4.1 %collective-permute-start = (f32[104,128]{1,0:T(8,128)S(1)}, f32[104,128]{1,0:T(8,128)S(1)}, u32[]{:S(2)}, u32[]{:S(2)}) collective-permute-start(f32[104,128]{1,0:T(8,128)S(1)} %get-tuple-element.39.rest_0_), channel_id=1, source_target_pairs={{0,4},{4,0},{8,12},{12,8},{16,20},{20,16},{24,28},{28,24},{1,5},{5... | collective-permute-start | bytes 159752 | tf_op jit(solution)/shard_map/ppermute | solution.py:56
  7.2 4.2 %collective-permute-start.1 = (f32[104,128]{1,0:T(8,128)S(1)}, f32[104,128]{1,0:T(8,128)S(1)}, u32[]{:S(2)}, u32[]{:S(2)}) collective-permute-start(f32[104,128]{1,0:T(8,128)S(1)} %get-tuple-element.39.rest_0_), channel_id=1, source_target_pairs={{0,8},{4,12},{8,0},{12,4},{16,24},{20,28},{24,16},{28,20},{1,9},{5... | collective-permute-start | bytes 159752 | tf_op jit(solution)/shard_map/ppermute | solution.py:56
  8.7 2.8 %collective-permute-start.6 = (f32[104,128]{1,0:T(8,128)S(1)}, f32[104,128]{1,0:T(8,128)S(1)}, u32[]{:S(2)}, u32[]{:S(2)}) collective-permute-start(f32[104,128]{1,0:T(8,128)S(1)} %collective-permute-done.4.rest_5_), channel_id=1, source_target_pairs={{0,8},{4,12},{8,0},{12,4},{16,24},{20,28},{24,16},{28,20},{1,9},{5... | collective-permute-start | bytes 159752 | tf_op jit(solution)/shard_map/ppermute | solution.py:56
  10.7 1.2 %collective-permute-start.5 = (f32[104,128]{1,0:T(8,128)S(1)}, f32[104,128]{1,0:T(8,128)S(1)}, u32[]{:S(2)}, u32[]{:S(2)}) collective-permute-start(f32[104,128]{1,0:T(8,128)S(1)} %collective-permute-done.3.rest_4_), channel_id=1, source_target_pairs={{0,8},{4,12},{8,0},{12,4},{16,24},{20,28},{24,16},{28,20},{1,9},{5... | collective-permute-start | bytes 159752 | tf_op jit(solution)/shard_map/ppermute | solution.py:56
  11.2 1.2 %collective-permute-start.2 = (f32[104,128]{1,0:T(8,128)S(1)}, f32[104,128]{1,0:T(8,128)S(1)}, u32[]{:S(2)}, u32[]{:S(2)}) collective-permute-start(f32[104,128]{1,0:T(8,128)S(1)} %collective-permute-done.rest_1_), channel_id=1, source_target_pairs={{0,8},{4,12},{8,0},{12,4},{16,24},{20,28},{24,16},{28,20},{1,9},{5... | collective-permute-start | bytes 159752 | tf_op jit(solution)/shard_map/ppermute | solution.py:56
  13.4 4.2 %collective-permute-start.12 = (f32[96,128]{1,0:T(8,128)S(1)}, f32[96,128]{1,0:T(8,128)S(1)}, u32[]{:S(2)}, u32[]{:S(2)}) collective-permute-start(f32[96,128]{1,0:T(8,128)S(1)} %get-tuple-element.59), channel_id=1, source_target_pairs={{0,16},{4,20},{8,24},{12,28},{16,0},{20,4},{24,8},{28,12},{1,17},{... | collective-permute-start | bytes 147464 | tf_op jit(solution)/shard_map/ppermute | solution.py:56
  15.0 4.1 %collective-permute-start.9 = (f32[64,128]{1,0:T(8,128)S(1)}, f32[64,128]{1,0:T(8,128)S(1)}, u32[]{:S(2)}, u32[]{:S(2)}) collective-permute-start(f32[64,128]{1,0:T(8,128)S(1)} %get-tuple-element.57), channel_id=1, source_target_pairs={{0,4},{4,0},{8,12},{12,8},{16,20},{20,16},{24,28},{28,24},{1,5},{5... | collective-permute-start | bytes 98312 | tf_op jit(solution)/shard_map/ppermute | solution.py:56
  15.5 12.9 %collective-permute-start.10 = (f32[96,128]{1,0:T(8,128)S(1)}, f32[96,128]{1,0:T(8,128)S(1)}, u32[]{:S(2)}, u32[]{:S(2)}) collective-permute-start(f32[96,128]{1,0:T(8,128)S(1)} %get-tuple-element.58), channel_id=1, source_target_pairs={{0,8},{4,12},{8,0},{12,4},{16,24},{20,28},{24,16},{28,20},{1,9},{5... | collective-permute-start | bytes 147464 | tf_op jit(solution)/shard_map/ppermute | solution.py:56
  17.5 10.9 %collective-permute-start.14 = (f32[96,128]{1,0:T(8,128)S(1)}, f32[96,128]{1,0:T(8,128)S(1)}, u32[]{:S(2)}, u32[]{:S(2)}) collective-permute-start(f32[96,128]{1,0:T(8,128)S(1)} %collective-permute-done.12.refs_16_), channel_id=1, source_target_pairs={{0,8},{4,12},{8,0},{12,4},{16,24},{20,28},{24,16},{28,20},{1,9},{5... | collective-permute-start | bytes 147464 | tf_op jit(solution)/shard_map/ppermute | solution.py:56
  17.5 4.6 %collective-permute-start.13 = (f32[32,128]{1,0:T(8,128)S(1)}, f32[32,128]{1,0:T(8,128)S(1)}, u32[]{:S(2)}, u32[]{:S(2)}) collective-permute-start(f32[32,128]{1,0:T(8,128)S(1)} %get-tuple-element.46.h_ref.refs_12_), channel_id=1, source_target_pairs={{0,20},{4,16},{8,28},{12,24},{16,4},{20,0},{24,12},{28,8},{1,21},{... | collective-permute-start | bytes 49160 | tf_op jit(solution)/shard_map/ppermute | solution.py:56
  19.0 9.3 %collective-permute-start.11 = (f32[64,128]{1,0:T(8,128)S(1)}, f32[64,128]{1,0:T(8,128)S(1)}, u32[]{:S(2)}, u32[]{:S(2)}) collective-permute-start(f32[64,128]{1,0:T(8,128)S(1)} %collective-permute-done.9.refs_13_), channel_id=1, source_target_pairs={{0,8},{4,12},{8,0},{12,4},{16,24},{20,28},{24,16},{28,20},{1,9},{5... | collective-permute-start | bytes 98312 | tf_op jit(solution)/shard_map/ppermute | solution.py:56
  22.2 6.2 %collective-permute-start.15 = (f32[32,128]{1,0:T(8,128)S(1)}, f32[32,128]{1,0:T(8,128)S(1)}, u32[]{:S(2)}, u32[]{:S(2)}) collective-permute-start(f32[32,128]{1,0:T(8,128)S(1)} %collective-permute-done.13.refs_17_), channel_id=1, source_target_pairs={{0,8},{4,12},{8,0},{12,4},{16,24},{20,28},{24,16},{28,20},{1,9},{5... | collective-permute-start | bytes 49160 | tf_op jit(solution)/shard_map/ppermute | solution.py:56
  22.2 3.6 %collective-permute-start.7 = (f32[2,512]{1,0:T(2,128)S(1)}, f32[2,512]{1,0:T(2,128)S(1)}, u32[]{:S(2)}, u32[]{:S(2)}) collective-permute-start(f32[2,512]{1,0:T(2,128)S(1)} %get-tuple-element.54), channel_id=1, source_target_pairs={{0,1},{1,0},{2,3},{3,2},{4,5},{5,4},{6,7},{7,6},{8,9},{9,8},{10,11... | collective-permute-start | bytes 12296 | tf_op jit(solution)/shard_map/ppermute | solution.py:107
  25.8 1.6 %collective-permute-start.8 = (f32[2,512]{1,0:T(2,128)S(1)}, f32[2,512]{1,0:T(2,128)S(1)}, u32[]{:S(2)}, u32[]{:S(2)}) collective-permute-start(f32[2,512]{1,0:T(2,128)S(1)} %get-tuple-element.55), channel_id=1, source_target_pairs={{0,8},{1,2},{2,1},{3,11},{4,12},{5,6},{6,5},{7,15},{8,0},{9,10},{1... | collective-permute-start | bytes 12296 | tf_op jit(solution)/shard_map/ppermute | solution.py:107
  30.2 7.4 %collective-permute-start.16 = (f32[1,32,128]{2,1,0:T(8,128)S(1)}, f32[1,32,128]{2,1,0:T(8,128)S(1)}, u32[]{:S(2)}, u32[]{:S(2)}) collective-permute-start(f32[1,32,128]{2,1,0:T(8,128)S(1)} %get-tuple-element.67), channel_id=1, source_target_pairs={{0,8},{1,9},{2,10},{3,11},{4,12},{5,13},{6,14},{7,15},{8,0},{9,1},... | collective-permute-start | bytes 49160 | tf_op jit(solution)/shard_map/ppermute | solution.py:107
  30.8 6.8 %collective-permute-start.17 = (f32[1,32,128]{2,1,0:T(8,128)S(1)}, f32[1,32,128]{2,1,0:T(8,128)S(1)}, u32[]{:S(2)}, u32[]{:S(2)}) collective-permute-start(f32[1,32,128]{2,1,0:T(8,128)S(1)} %get-tuple-element.68), channel_id=1, source_target_pairs={{0,24},{1,25},{2,26},{3,27},{4,28},{5,29},{6,30},{7,31},{8,16},{9,... | collective-permute-start | bytes 49160 | tf_op jit(solution)/shard_map/ppermute | solution.py:107
  32.0 5.6 %collective-permute-start.18 = (f32[1,16,128]{2,1,0:T(8,128)S(1)}, f32[1,16,128]{2,1,0:T(8,128)S(1)}, u32[]{:S(2)}, u32[]{:S(2)}) collective-permute-start(f32[1,16,128]{2,1,0:T(8,128)S(1)} %get-tuple-element.69), channel_id=1, source_target_pairs={{0,4},{1,5},{2,6},{3,7},{4,0},{5,1},{6,2},{7,3},{8,12},{9,13},{10,... | collective-permute-start | bytes 24584 | tf_op jit(solution)/shard_map/ppermute | solution.py:107
  32.5 5.1 %collective-permute-start.19 = (f32[1,512]{1,0:T(1,128)S(1)}, f32[1,512]{1,0:T(1,128)S(1)}, u32[]{:S(2)}, u32[]{:S(2)}) collective-permute-start(f32[1,512]{1,0:T(1,128)S(1)} %get-tuple-element.70), channel_id=1, source_target_pairs={{0,1},{1,0},{2,3},{3,2},{4,5},{5,4},{6,7},{7,6},{8,9},{9,8},{10,11... | collective-permute-start | bytes 6152 | tf_op jit(solution)/shard_map/ppermute | solution.py:107
  36.0 1.6 %collective-permute-start.20 = (f32[1,512]{1,0:T(1,128)S(1)}, f32[1,512]{1,0:T(1,128)S(1)}, u32[]{:S(2)}, u32[]{:S(2)}) collective-permute-start(f32[1,512]{1,0:T(1,128)S(1)} %get-tuple-element.71), channel_id=1, source_target_pairs={{0,8},{1,2},{2,1},{3,11},{4,12},{5,6},{6,5},{7,15},{8,0},{9,10},{1... | collective-permute-start | bytes 6152 | tf_op jit(solution)/shard_map/ppermute | solution.py:107
where the time goes:
time: 38.7 us; the launch traced here: 38.5 us
  starting transfers between devices  15.9 us (41%)
  waiting for transfers between devices  13.2 us (34%)
  Pallas kernels  8.67 us (22%)
  between operations  0.77 us (2%)
    ppermute x14, waiting for transfers between devices, swap(): return lax.ppermute(x, GROUP, [(i, i ^ k) for i in range(n)])  9.96 us
    pallas_call x10, Pallas kernels, call(): pl.pallas_call(body, out_shape=out_shape, in_specs=[pl.BlockSpec(memory_s...  8.67 us
    ppermute x14, starting transfers between devices, swap(): return lax.ppermute(x, GROUP, [(i, i ^ k) for i in range(n)])  8.49 us
    ppermute x7, starting transfers between devices, exchange(): out.append(lax.ppermute(face, AXES, swap_list(axis, r)))  7.38 us
    ppermute x7, waiting for transfers between devices, exchange(): out.append(lax.ppermute(face, AXES, swap_list(axis, r)))  3.21 us
  transfers between devices with their start and end apart: 21, of which 9 were waited for; matrix products, arithmetic and copies ran while one was open for 0% of the time, Pallas kernels for 8%

commit v1 on v0

--- a/solution.py
+++ b/solution.py
@@ -41,6 +41,15 @@
     return lax.dot_general(
         a, b, (((ca,), (cb,)), ((), ())), precision=precision, preferred_element_type=F32
     )
+
+
+def split(x):
+    hi = x.astype(BF16)
+    return hi, (x - hi.astype(F32)).astype(BF16)
+
+
+def dot3(a, b, ca, cb):
+    return dot(a[0], b[0], ca, cb) + (dot(a[0], b[1], ca, cb) + dot(a[1], b[0], ca, cb))
 
 
 def group_size():
@@ -247,30 +256,37 @@
         for copy in copies[5 + chunks :]:
             copy.wait()
 
-    def rock(t_ref, c_ref, *faces):
-        write_faces(faces, specs2, (t_ref[...], c_ref[...]))
-
-    def both(w_ref, a_ref, *rest):
+    def own_mix(table, mix_ref):
+        ids = table[:links, :].astype(jnp.int32)
+        if pairs:
+            ids = ids ^ ((lax.axis_index("gx") * low + lax.axis_index("gy")) * nb)
+        mix = split(mix_of(ids, table[links : 2 * links, :]).T[:nb, :])
+        mix_ref[0], mix_ref[1] = mix
+
+    def rock(t_ref, c_ref, send_ref, *outs):
+        write_faces(outs[1:], specs2, (t_ref[...], c_ref[...]))
+        own_mix(send_ref[3 * nb :, :], outs[0])
+
+    def both(w_ref, a_ref, mix_ref, *rest):
         slots, rest = rest[:n], rest[n:]
-        faces, (h_ref, mix_ref, *sends) = rest[: len(xy)], rest[len(xy) :]
+        faces, (h_ref, *sends) = rest[: len(xy)], rest[len(xy) :]
         me = lax.axis_index("gx") * low + lax.axis_index("gy")
-        heads = jnp.concatenate([s[:nb, :] for s in slots], axis=0)
+        heads = split(jnp.concatenate([s[:nb, :] for s in slots], axis=0))
         per = tri // nb
-        first = []
+        tables = []
         for g in range(0, n, per):
             table = slots[g][3 * nb :, :]
             for i in range(1, per):
                 table = table + pltpu.roll(slots[g + i][3 * nb :, :], i * nb, 1)
-            ids = table[:links, :].astype(jnp.int32) ^ (me * nb)
-            mix = mix_of(ids, table[links : 2 * links, :])
-            if g == 0:
-                mix_ref[...] = mix
-            across = dot(mix, heads, 0, 0, HIGH)
-            for i in range(per):
-                s = slots[g + i]
-                first.append((s[nb : 2 * nb, :] + across[i * nb : (i + 1) * nb, :]) / s[2 * nb : 3 * nb, :])
+            tables.append(table)
+        table = jnp.concatenate(tables, axis=1)
+        ids = table[:links, :].astype(jnp.int32) ^ (me * nb)
+        across = dot3(split(mix_of(ids, table[links : 2 * links, :])), heads, 0, 0)
+        first = []
+        for k, s in enumerate(slots):
+            first.append((s[nb : 2 * nb, :] + across[k * nb : (k + 1) * nb, :]) / s[2 * nb : 3 * nb, :])
         inner = inner_of(a_ref, first[0])
-        across = dot(mix_ref[...], jnp.concatenate(first, axis=0), 0, 0, HIGH)[:nb, :]
+        across = dot3(mix_ref, split(jnp.concatenate(first, axis=0)), 1, 0)
         h = (w_ref[...] + inner + across) / slots[0][2 * nb : 3 * nb, :]
         h_ref[...] = h
         for send, face in zip(sends, faces):
@@ -283,7 +299,7 @@
         o_ref[...] = inner_of(a_ref, h_ref[...])
 
     def sweep(w_ref, den_ref, mix_ref, inner_ref, heads):
-        across = dot(mix_ref[...], heads, 0, 0, HIGH)[:nb, :]
+        across = dot3(mix_ref, split(heads), 1, 0)
         return (w_ref[...] + inner_ref[...] + across) / den_ref[...]
 
     def gather(first, t_ref, hv_ref, liq_ref, tf_ref, q_ref, hot_ref):
@@ -396,17 +412,18 @@
     )
     if pairs:
         slots = meet({k: send for k in range(n - 1, 0, -1) if not k & low}, send)
-    faces = call(rock, [sds(s) for _, _, s in specs2], t, c)
+    mix, *faces = call(rock, [sds((2, nb, n * nb), BF16)] + [sds(s) for _, _, s in specs2], t, c, send)
     got_z = exchange([faces[i] for i in zs], [specs2[i] for i in zs])
     if pairs:
         y_at, xa_at, xb_at = 1, low, 2 * low
         order = {"gx": (xa_at, xb_at), "gy": (y_at,)}
         rides = [order[specs2[i][0]][specs2[i][1]] for i in xy]
-        h, mix, *sends = call(
+        h, *sends = call(
             both,
-            [blk, sds((n * nb, tri))] + [sds((nb + 2 * specs2[i][2][1], tri)) for i in xy],
+            [blk] + [sds((nb + 2 * specs2[i][2][1], tri)) for i in xy],
             w,
             a,
+            mix,
             send,
             *[slots[k] for k in range(1, n)],
             *[faces[i] for i in xy],
@@ -426,16 +443,10 @@
     else:
         den = send[2 * nb : 3 * nb]
         h = initial_hydraulic_head
-        ids = jnp.zeros((small, tri), jnp.int32).at[:links, :nb].set(crossing_partner_number.T)
-        perm = send[3 * nb + links : 3 * nb + 2 * links]
-
-        def mix_body(ids_ref, perm_ref, mix_ref):
-            mix_ref[...] = mix_of(ids_ref[...], perm_ref[...])
 
         def sweep_body(w_ref, den_ref, mix_ref, inner_ref, heads_ref, h_ref):
             h_ref[...] = sweep(w_ref, den_ref, mix_ref, inner_ref, heads_ref[...])
 
-        mix = call(mix_body, sds((n * nb, tri)), ids[:links], perm)
         for _ in range(SWEEPS - 1):
             heads = lax.all_gather(h, GROUP, axis=0, tiled=True)
             inner = call(inner_body, blk, a, h)

time: 38.7 us -> 38.4 us (level)
  no operation moved by 1% of the time
where the time goes in v1:
time: 38.4 us; the launch traced here: 38.2 us
  starting transfers between devices  15.9 us (41%)
  waiting for transfers between devices  13.1 us (34%)
  Pallas kernels  8.42 us (22%)
  between operations  0.77 us (2%)
    ppermute x14, waiting for transfers between devices, swap(): return lax.ppermute(x, GROUP, [(i, i ^ k) for i in range(n)])  9.94 us
    ppermute x14, starting transfers between devices, swap(): return lax.ppermute(x, GROUP, [(i, i ^ k) for i in range(n)])  8.49 us
    pallas_call x10, Pallas kernels, call(): pl.pallas_call(body, out_shape=out_shape, in_specs=[pl.BlockSpec(memory_s...  8.42 us
    ppermute x7, starting transfers between devices, exchange(): out.append(lax.ppermute(face, AXES, swap_list(axis, r)))  7.39 us
    ppermute x7, waiting for transfers between devices, exchange(): out.append(lax.ppermute(face, AXES, swap_list(axis, r)))  3.21 us
  transfers between devices with their start and end apart: 21, of which 9 were waited for; matrix products, arithmetic and copies ran while one was open for 0% of the time, Pallas kernels for 8%

profile of v1, /device:TPU:0, one launch (start us, length us, event | category | flops | bytes accessed | tf_op | source)
XLA Modules:
  0.0 38.2 jit_solution(17459830823245410978)
XLA Ops:
  0.6 1.9 %shard_map.122 = (f32[104,128]{1,0:T(8,128)S(1)}, f32[32,128]{1,0:T(8,128)S(1)}, f32[16,32,128]{2,1,0:T(8,128)S(1)}, f32[16,32,128]{2,1,0:T(8,128)S(1)}, s32[32,...) custom-call(s32[4,32]{1,0:T(4,128)} %bitcast.2, ...), custom_call_target="tpu_custom_call" | custom-call | tf_op jit(solution)/shard_map/pallas_call | solution.py:23
  2.6 4.0 %collective-permute-start.4 = (f32[104,128]{1,0:T(8,128)S(1)}, f32[104,128]{1,0:T(8,128)S(1)}, u32[]{:S(2)}, u32[]{:S(2)}) collective-permute-start(f32[104,128]{1,0:T(8,128)S(1)} %get-tuple-element.39.send_ref.rest_0_), channel_id=1, source_target_pairs={{0,20},{4,16},{8,28},{12,24},{16,4},{20,0},{24,12},{28,8},{1,21},{... | collective-permute-start | bytes 159752 | tf_op jit(solution)/shard_map/ppermute | solution.py:65
  6.5 0.5 %collective-permute-start.3 = (f32[104,128]{1,0:T(8,128)S(1)}, f32[104,128]{1,0:T(8,128)S(1)}, u32[]{:S(2)}, u32[]{:S(2)}) collective-permute-start(f32[104,128]{1,0:T(8,128)S(1)} %get-tuple-element.39.send_ref.rest_0_), channel_id=1, source_target_pairs={{0,16},{4,20},{8,24},{12,28},{16,0},{20,4},{24,8},{28,12},{1,17},{... | collective-permute-start | bytes 159752 | tf_op jit(solution)/shard_map/ppermute | solution.py:65
  7.0 0.1 collective-permute-start
  7.2 0.0 collective-permute-start.1
  7.2 1.5 %collective-permute-done.4.rest_5_ = f32[104,128]{1,0:T(8,128)S(1)} collective-permute-done((f32[104,128]{1,0:T(8,128)S(1)}, f32[104,128]{1,0:T(8,128)S(1)}, u32[]{:S(2)}, u32[]{:S(2)}) %collective-permute-start.4) | collective-permute-done | bytes 53280 | tf_op jit(solution)/shard_map/ppermute | solution.py:65
  8.7 0.0 collective-permute-start.6
  8.7 2.0 %collective-permute-done.3.rest_4_ = f32[104,128]{1,0:T(8,128)S(1)} collective-permute-done((f32[104,128]{1,0:T(8,128)S(1)}, f32[104,128]{1,0:T(8,128)S(1)}, u32[]{:S(2)}, u32[]{:S(2)}) %collective-permute-start.3) | collective-permute-done | bytes 53280 | tf_op jit(solution)/shard_map/ppermute | solution.py:65
  10.7 0.0 collective-permute-start.5
  10.7 0.5 %collective-permute-done.rest_1_ = f32[104,128]{1,0:T(8,128)S(1)} collective-permute-done((f32[104,128]{1,0:T(8,128)S(1)}, f32[104,128]{1,0:T(8,128)S(1)}, u32[]{:S(2)}, u32[]{:S(2)}) %collective-permute-start) | collective-permute-done | bytes 53280 | tf_op jit(solution)/shard_map/ppermute | solution.py:65
  11.2 0.0 collective-permute-start.2
  11.2 0.2 shard_map.123
  11.4 0.0 collective-permute-done.1.rest_2_
  11.4 0.0 collective-permute-done.6.rest_7_
  11.4 0.5 %collective-permute-done.5.rest_6_ = f32[104,128]{1,0:T(8,128)S(1)} collective-permute-done((f32[104,128]{1,0:T(8,128)S(1)}, f32[104,128]{1,0:T(8,128)S(1)}, u32[]{:S(2)}, u32[]{:S(2)}) %collective-permute-start.5) | collective-permute-done | bytes 53280 | tf_op jit(solution)/shard_map/ppermute | solution.py:65
  11.9 0.5 %collective-permute-done.2.rest_3_ = f32[104,128]{1,0:T(8,128)S(1)} collective-permute-done((f32[104,128]{1,0:T(8,128)S(1)}, f32[104,128]{1,0:T(8,128)S(1)}, u32[]{:S(2)}, u32[]{:S(2)}) %collective-permute-start.2) | collective-permute-done | bytes 53280 | tf_op jit(solution)/shard_map/ppermute | solution.py:65
  12.4 0.8 %shard_map.124 = (f32[32,128]{1,0:T(8,128)S(1)}, f32[96,128]{1,0:T(8,128)S(1)}, f32[96,128]{1,0:T(8,128)S(1)}, f32[64,128]{1,0:T(8,128)S(1)}) custom-call(f32[32,128]{1,0:T(8,128)S(1)} %get-tuple-element.41.w_ref.refs_2_, bf16[32,128,128]{2,1,0:T(8,128)(2,1)S(1)} %get-tuple-element.42.a_ref, bf16[2,32,256]{2,1,0:T(8,128)(2,1)S(1)} %get-tuple-element.40.mix_ref.refs_0_, ...), custom_call_target="tpu_custom_call" | custom-call | tf_op jit(solution)/shard_map/pallas_call | solution.py:23
  13.3 1.6 %collective-permute-start.12 = (f32[96,128]{1,0:T(8,128)S(1)}, f32[96,128]{1,0:T(8,128)S(1)}, u32[]{:S(2)}, u32[]{:S(2)}) collective-permute-start(f32[96,128]{1,0:T(8,128)S(1)} %get-tuple-element.59), channel_id=1, source_target_pairs={{0,16},{4,20},{8,24},{12,28},{16,0},{20,4},{24,8},{28,12},{1,17},{... | collective-permute-start | bytes 147464 | tf_op jit(solution)/shard_map/ppermute | solution.py:65
  14.9 0.5 %collective-permute-start.9 = (f32[64,128]{1,0:T(8,128)S(1)}, f32[64,128]{1,0:T(8,128)S(1)}, u32[]{:S(2)}, u32[]{:S(2)}) collective-permute-start(f32[64,128]{1,0:T(8,128)S(1)} %get-tuple-element.57), channel_id=1, source_target_pairs={{0,4},{4,0},{8,12},{12,8},{16,20},{20,16},{24,28},{28,24},{1,5},{5... | collective-permute-start | bytes 98312 | tf_op jit(solution)/shard_map/ppermute | solution.py:65
  15.4 0.0 collective-permute-start.10
  15.4 2.0 %collective-permute-done.12.refs_16_ = f32[96,128]{1,0:T(8,128)S(1)} collective-permute-done((f32[96,128]{1,0:T(8,128)S(1)}, f32[96,128]{1,0:T(8,128)S(1)}, u32[]{:S(2)}, u32[]{:S(2)}) %collective-permute-start.12) | collective-permute-done | bytes 49184 | tf_op jit(solution)/shard_map/ppermute | solution.py:65
  17.4 0.0 collective-permute-start.14
  17.4 1.5 %collective-permute-start.13 = (f32[32,128]{1,0:T(8,128)S(1)}, f32[32,128]{1,0:T(8,128)S(1)}, u32[]{:S(2)}, u32[]{:S(2)}) collective-permute-start(f32[32,128]{1,0:T(8,128)S(1)} %get-tuple-element.46.h_ref.refs_12_), channel_id=1, source_target_pairs={{0,20},{4,16},{8,28},{12,24},{16,4},{20,0},{24,12},{28,8},{1,21},{... | collective-permute-start | bytes 49160 | tf_op jit(solution)/shard_map/ppermute | solution.py:65
  18.9 0.0 collective-permute-done.9.refs_13_
  18.9 0.2 collective-permute-start.11
  19.1 2.9 %collective-permute-done.13.refs_17_ = f32[32,128]{1,0:T(8,128)S(1)} collective-permute-done((f32[32,128]{1,0:T(8,128)S(1)}, f32[32,128]{1,0:T(8,128)S(1)}, u32[]{:S(2)}, u32[]{:S(2)}) %collective-permute-start.13) | collective-permute-done | bytes 16416 | tf_op jit(solution)/shard_map/ppermute | solution.py:65
  22.1 0.0 collective-permute-start.15
  22.1 1.6 %collective-permute-start.7 = (f32[2,512]{1,0:T(2,128)S(1)}, f32[2,512]{1,0:T(2,128)S(1)}, u32[]{:S(2)}, u32[]{:S(2)}) collective-permute-start(f32[2,512]{1,0:T(2,128)S(1)} %get-tuple-element.54), channel_id=1, source_target_pairs={{0,1},{1,0},{2,3},{3,2},{4,5},{5,4},{6,7},{7,6},{8,9},{9,8},{10,11... | collective-permute-start | bytes 12296 | tf_op jit(solution)/shard_map/ppermute | solution.py:116
  23.6 2.0 %collective-permute-done.7.rest_0_ = f32[2,512]{1,0:T(2,128)S(1)} collective-permute-done((f32[2,512]{1,0:T(2,128)S(1)}, f32[2,512]{1,0:T(2,128)S(1)}, u32[]{:S(2)}, u32[]{:S(2)}) %collective-permute-start.7) | collective-permute-done | bytes 4128 | tf_op jit(solution)/shard_map/ppermute | solution.py:116
  25.7 0.0 collective-permute-start.8
  25.7 0.8 %shard_map.127 = (f32[16,128]{1,0:T(8,128)S(1)}, bf16[512,2048]{1,0:T(8,128)(2,1)S(1)}) custom-call(f32[16,32,128]{2,1,0:T(8,128)S(1)} %get-tuple-element.37.t_ref.refs_10_, s32[32,128]{1,0:T(8,128)S(1)} %get-tuple-element.47.hv_ref.refs_6_, f32[32,128]{1,0:T(8,128)S(1)} %get-tuple-element.48.liq_ref, f32[32,128]{1,0:T(8,128)S(1)} %get-tuple-element.49.tf_ref), custom_call_target="tpu_custom_call" | custom-call | tf_op jit(solution)/shard_map/pallas_call | solution.py:23
  26.5 0.8 %shard_map.126 = (f32[16,128]{1,0:T(8,128)S(1)}, bf16[512,2048]{1,0:T(8,128)(2,1)S(1)}) custom-call(f32[16,32,128]{2,1,0:T(8,128)S(1)} %get-tuple-element.37.t_ref.refs_10_, s32[32,128]{1,0:T(8,128)S(1)} %get-tuple-element.47.hv_ref.refs_6_, f32[32,128]{1,0:T(8,128)S(1)} %get-tuple-element.48.liq_ref, f32[32,128]{1,0:T(8,128)S(1)} %get-tuple-element.49.tf_ref), custom_call_target="tpu_custom_call" | custom-call | tf_op jit(solution)/shard_map/pallas_call | solution.py:23
  27.3 0.0 collective-permute-done.8.rest_1_
  27.3 0.6 %shard_map.128 = (f32[16,32,128]{2,1,0:T(8,128)S(1)}, f32[16,32,128]{2,1,0:T(8,128)S(1)}, f32[16,32,128]{2,1,0:T(8,128)S(1)}) custom-call(f32[16,32,128]{2,1,0:T(8,128)S(1)} %get-tuple-element.37.t_ref.refs_10_, f32[16,32,128]{2,1,0:T(8,128)S(1)} %get-tuple-element.38.c_ref.refs_11_, f32[2,512]{1,0:T(2,128)S(1)} %collective-permute-done.7.rest_0_, ...), custom_call_target="tpu_custom_call" | custom-call | tf_op jit(solution)/shard_map/pallas_call | solution.py:23
  27.9 0.4 shard_map.125.refs_3_
  28.2 0.0 collective-permute-done.15.refs_19_
  28.2 0.0 collective-permute-done.10.refs_14_
  28.3 0.0 collective-permute-done.11.refs_15_
  28.3 0.0 collective-permute-done.14.refs_18_
  28.3 1.7 %shard_map.129 = (f32[32,128]{1,0:T(8,128)S(1)}, f32[16,32,128]{2,1,0:T(8,128)S(1)}, f32[16,32,128]{2,1,0:T(8,128)S(1)}, f32[2,32,128]{2,1,0:T(8,128)S(1)}, f32[...) custom-call(bf16[2,32,256]{2,1,0:T(8,128)(2,1)S(1)} %get-tuple-eleme, ...), custom_call_target="tpu_custom_call" | custom-call | tf_op jit(solution)/shard_map/pallas_call | solution.py:23
  29.9 0.6 %collective-permute-start.16 = (f32[1,32,128]{2,1,0:T(8,128)S(1)}, f32[1,32,128]{2,1,0:T(8,128)S(1)}, u32[]{:S(2)}, u32[]{:S(2)}) collective-permute-start(f32[1,32,128]{2,1,0:T(8,128)S(1)} %get-tuple-element.67), channel_id=1, source_target_pairs={{0,8},{1,9},{2,10},{3,11},{4,12},{5,13},{6,14},{7,15},{8,0},{9,1},... | collective-permute-start | bytes 49160 | tf_op jit(solution)/shard_map/ppermute | solution.py:116
  30.5 1.2 %collective-permute-start.17 = (f32[1,32,128]{2,1,0:T(8,128)S(1)}, f32[1,32,128]{2,1,0:T(8,128)S(1)}, u32[]{:S(2)}, u32[]{:S(2)}) collective-permute-start(f32[1,32,128]{2,1,0:T(8,128)S(1)} %get-tuple-element.68), channel_id=1, source_target_pairs={{0,24},{1,25},{2,26},{3,27},{4,28},{5,29},{6,30},{7,31},{8,16},{9,... | collective-permute-start | bytes 49160 | tf_op jit(solution)/shard_map/ppermute | solution.py:116
  31.7 0.5 %collective-permute-start.18 = (f32[1,16,128]{2,1,0:T(8,128)S(1)}, f32[1,16,128]{2,1,0:T(8,128)S(1)}, u32[]{:S(2)}, u32[]{:S(2)}) collective-permute-start(f32[1,16,128]{2,1,0:T(8,128)S(1)} %get-tuple-element.69), channel_id=1, source_target_pairs={{0,4},{1,5},{2,6},{3,7},{4,0},{5,1},{6,2},{7,3},{8,12},{9,13},{10,... | collective-permute-start | bytes 24584 | tf_op jit(solution)/shard_map/ppermute | solution.py:116
  32.3 3.5 %collective-permute-start.19 = (f32[1,512]{1,0:T(1,128)S(1)}, f32[1,512]{1,0:T(1,128)S(1)}, u32[]{:S(2)}, u32[]{:S(2)}) collective-permute-start(f32[1,512]{1,0:T(1,128)S(1)} %get-tuple-element.70), channel_id=1, source_target_pairs={{0,1},{1,0},{2,3},{3,2},{4,5},{5,4},{6,7},{7,6},{8,9},{9,8},{10,11... | collective-permute-start | bytes 6152 | tf_op jit(solution)/shard_map/ppermute | solution.py:116
  35.8 0.0 collective-permute-start.20
  35.8 0.4 %shard_map.130.v_ref = f32[16,32,128]{2,1,0:T(8,128)S(1)} custom-call(f32[16,32,128]{2,1,0:T(8,128)S(1)} %get-tuple-element.61.t_ref, f32[16,32,128]{2,1,0:T(8,128)S(1)} %get-tuple-element.62.f_ref, f32[16,32,128]{2,1,0:T(8,128)S(1)} %get-tuple-element.38.c_ref.refs_11_, f32[16,32,128]{2,1,0:T(8,128)S(1)} %get-tuple-element.63.keep_ref), custom_call_target="tpu_custom_call" | custom-call | tf_op jit(solution)/shard_map/pallas_call | solution.py:23
  36.1 1.2 %collective-permute-done.19.rest_3_ = f32[1,512]{1,0:T(1,128)S(1)} collective-permute-done((f32[1,512]{1,0:T(1,128)S(1)}, f32[1,512]{1,0:T(1,128)S(1)}, u32[]{:S(2)}, u32[]{:S(2)}) %collective-permute-start.19) | collective-permute-done | bytes 2080 | tf_op jit(solution)/shard_map/ppermute | solution.py:116
  37.3 0.0 collective-permute-done.20.rest_4_
  37.3 0.0 collective-permute-done.18.rest_2_
  37.3 0.0 collective-permute-done.16.rest_0_
  37.3 0.0 collective-permute-done.17.rest_1_
  37.3 0.9 %shard_map.131 = (f32[32,128]{1,0:T(8,128)}, f32[16,32,128]{2,1,0:T(8,128)}) custom-call(f32[32,128]{1,0:T(8,128)S(1)} %get-tuple-element.60.h_ref, f32[16,32,128]{2,1,0:T(8,128)S(1)} %shard_map.130.v_ref, f32[16,32,128]{2,1,0:T(8,128)S(1)} %get-tuple-element.61.t_ref, f32[2,32,128]{2,1,0:T(8,128)S(1)} %get-tuple-element.64.wx_ref, ...), custom_call_target="tpu_custom_call" | custom-call | tf_op jit(solution)/shard_map/pallas_call | solution.py:23
  (1 shorter events, 0.0 us)
Async XLA Ops:
  2.6 6.1 %collective-permute-start.4 = (f32[104,128]{1,0:T(8,128)S(1)}, f32[104,128]{1,0:T(8,128)S(1)}, u32[]{:S(2)}, u32[]{:S(2)}) collective-permute-start(f32[104,128]{1,0:T(8,128)S(1)} %get-tuple-element.39.send_ref.rest_0_), channel_id=1, source_target_pairs={{0,20},{4,16},{8,28},{12,24},{16,4},{20,0},{24,12},{28,8},{1,21},{... | collective-permute-start | bytes 159752 | tf_op jit(solution)/shard_map/ppermute | solution.py:65
  6.5 4.1 %collective-permute-start.3 = (f32[104,128]{1,0:T(8,128)S(1)}, f32[104,128]{1,0:T(8,128)S(1)}, u32[]{:S(2)}, u32[]{:S(2)}) collective-permute-start(f32[104,128]{1,0:T(8,128)S(1)} %get-tuple-element.39.send_ref.rest_0_), channel_id=1, source_target_pairs={{0,16},{4,20},{8,24},{12,28},{16,0},{20,4},{24,8},{28,12},{1,17},{... | collective-permute-start | bytes 159752 | tf_op jit(solution)/shard_map/ppermute | solution.py:65
  7.0 4.1 %collective-permute-start = (f32[104,128]{1,0:T(8,128)S(1)}, f32[104,128]{1,0:T(8,128)S(1)}, u32[]{:S(2)}, u32[]{:S(2)}) collective-permute-start(f32[104,128]{1,0:T(8,128)S(1)} %get-tuple-element.39.send_ref.rest_0_), channel_id=1, source_target_pairs={{0,4},{4,0},{8,12},{12,8},{16,20},{20,16},{24,28},{28,24},{1,5},{5... | collective-permute-start | bytes 159752 | tf_op jit(solution)/shard_map/ppermute | solution.py:65
  7.2 4.2 %collective-permute-start.1 = (f32[104,128]{1,0:T(8,128)S(1)}, f32[104,128]{1,0:T(8,128)S(1)}, u32[]{:S(2)}, u32[]{:S(2)}) collective-permute-start(f32[104,128]{1,0:T(8,128)S(1)} %get-tuple-element.39.send_ref.rest_0_), channel_id=1, source_target_pairs={{0,8},{4,12},{8,0},{12,4},{16,24},{20,28},{24,16},{28,20},{1,9},{5... | collective-permute-start | bytes 159752 | tf_op jit(solution)/shard_map/ppermute | solution.py:65
  8.7 2.8 %collective-permute-start.6 = (f32[104,128]{1,0:T(8,128)S(1)}, f32[104,128]{1,0:T(8,128)S(1)}, u32[]{:S(2)}, u32[]{:S(2)}) collective-permute-start(f32[104,128]{1,0:T(8,128)S(1)} %collective-permute-done.4.rest_5_), channel_id=1, source_target_pairs={{0,8},{4,12},{8,0},{12,4},{16,24},{20,28},{24,16},{28,20},{1,9},{5... | collective-permute-start | bytes 159752 | tf_op jit(solution)/shard_map/ppermute | solution.py:65
  10.7 1.2 %collective-permute-start.5 = (f32[104,128]{1,0:T(8,128)S(1)}, f32[104,128]{1,0:T(8,128)S(1)}, u32[]{:S(2)}, u32[]{:S(2)}) collective-permute-start(f32[104,128]{1,0:T(8,128)S(1)} %collective-permute-done.3.rest_4_), channel_id=1, source_target_pairs={{0,8},{4,12},{8,0},{12,4},{16,24},{20,28},{24,16},{28,20},{1,9},{5... | collective-permute-start | bytes 159752 | tf_op jit(solution)/shard_map/ppermute | solution.py:65
  11.2 1.2 %collective-permute-start.2 = (f32[104,128]{1,0:T(8,128)S(1)}, f32[104,128]{1,0:T(8,128)S(1)}, u32[]{:S(2)}, u32[]{:S(2)}) collective-permute-start(f32[104,128]{1,0:T(8,128)S(1)} %collective-permute-done.rest_1_), channel_id=1, source_target_pairs={{0,8},{4,12},{8,0},{12,4},{16,24},{20,28},{24,16},{28,20},{1,9},{5... | collective-permute-start | bytes 159752 | tf_op jit(solution)/shard_map/ppermute | solution.py:65
  13.3 4.2 %collective-permute-start.12 = (f32[96,128]{1,0:T(8,128)S(1)}, f32[96,128]{1,0:T(8,128)S(1)}, u32[]{:S(2)}, u32[]{:S(2)}) collective-permute-start(f32[96,128]{1,0:T(8,128)S(1)} %get-tuple-element.59), channel_id=1, source_target_pairs={{0,16},{4,20},{8,24},{12,28},{16,0},{20,4},{24,8},{28,12},{1,17},{... | collective-permute-start | bytes 147464 | tf_op jit(solution)/shard_map/ppermute | solution.py:65
  14.9 4.1 %collective-permute-start.9 = (f32[64,128]{1,0:T(8,128)S(1)}, f32[64,128]{1,0:T(8,128)S(1)}, u32[]{:S(2)}, u32[]{:S(2)}) collective-permute-start(f32[64,128]{1,0:T(8,128)S(1)} %get-tuple-element.57), channel_id=1, source_target_pairs={{0,4},{4,0},{8,12},{12,8},{16,20},{20,16},{24,28},{28,24},{1,5},{5... | collective-permute-start | bytes 98312 | tf_op jit(solution)/shard_map/ppermute | solution.py:65
  15.4 12.9 %collective-permute-start.10 = (f32[96,128]{1,0:T(8,128)S(1)}, f32[96,128]{1,0:T(8,128)S(1)}, u32[]{:S(2)}, u32[]{:S(2)}) collective-permute-start(f32[96,128]{1,0:T(8,128)S(1)} %get-tuple-element.58), channel_id=1, source_target_pairs={{0,8},{4,12},{8,0},{12,4},{16,24},{20,28},{24,16},{28,20},{1,9},{5... | collective-permute-start | bytes 147464 | tf_op jit(solution)/shard_map/ppermute | solution.py:65
  17.4 10.9 %collective-permute-start.14 = (f32[96,128]{1,0:T(8,128)S(1)}, f32[96,128]{1,0:T(8,128)S(1)}, u32[]{:S(2)}, u32[]{:S(2)}) collective-permute-start(f32[96,128]{1,0:T(8,128)S(1)} %collective-permute-done.12.refs_16_), channel_id=1, source_target_pairs={{0,8},{4,12},{8,0},{12,4},{16,24},{20,28},{24,16},{28,20},{1,9},{5... | collective-permute-start | bytes 147464 | tf_op jit(solution)/shard_map/ppermute | solution.py:65
  17.4 4.6 %collective-permute-start.13 = (f32[32,128]{1,0:T(8,128)S(1)}, f32[32,128]{1,0:T(8,128)S(1)}, u32[]{:S(2)}, u32[]{:S(2)}) collective-permute-start(f32[32,128]{1,0:T(8,128)S(1)} %get-tuple-element.46.h_ref.refs_12_), channel_id=1, source_target_pairs={{0,20},{4,16},{8,28},{12,24},{16,4},{20,0},{24,12},{28,8},{1,21},{... | collective-permute-start | bytes 49160 | tf_op jit(solution)/shard_map/ppermute | solution.py:65
  18.9 9.3 %collective-permute-start.11 = (f32[64,128]{1,0:T(8,128)S(1)}, f32[64,128]{1,0:T(8,128)S(1)}, u32[]{:S(2)}, u32[]{:S(2)}) collective-permute-start(f32[64,128]{1,0:T(8,128)S(1)} %collective-permute-done.9.refs_13_), channel_id=1, source_target_pairs={{0,8},{4,12},{8,0},{12,4},{16,24},{20,28},{24,16},{28,20},{1,9},{5... | collective-permute-start | bytes 98312 | tf_op jit(solution)/shard_map/ppermute | solution.py:65
  22.1 6.2 %collective-permute-start.15 = (f32[32,128]{1,0:T(8,128)S(1)}, f32[32,128]{1,0:T(8,128)S(1)}, u32[]{:S(2)}, u32[]{:S(2)}) collective-permute-start(f32[32,128]{1,0:T(8,128)S(1)} %collective-permute-done.13.refs_17_), channel_id=1, source_target_pairs={{0,8},{4,12},{8,0},{12,4},{16,24},{20,28},{24,16},{28,20},{1,9},{5... | collective-permute-start | bytes 49160 | tf_op jit(solution)/shard_map/ppermute | solution.py:65
  22.1 3.6 %collective-permute-start.7 = (f32[2,512]{1,0:T(2,128)S(1)}, f32[2,512]{1,0:T(2,128)S(1)}, u32[]{:S(2)}, u32[]{:S(2)}) collective-permute-start(f32[2,512]{1,0:T(2,128)S(1)} %get-tuple-element.54), channel_id=1, source_target_pairs={{0,1},{1,0},{2,3},{3,2},{4,5},{5,4},{6,7},{7,6},{8,9},{9,8},{10,11... | collective-permute-start | bytes 12296 | tf_op jit(solution)/shard_map/ppermute | solution.py:116
  25.7 1.6 %collective-permute-start.8 = (f32[2,512]{1,0:T(2,128)S(1)}, f32[2,512]{1,0:T(2,128)S(1)}, u32[]{:S(2)}, u32[]{:S(2)}) collective-permute-start(f32[2,512]{1,0:T(2,128)S(1)} %get-tuple-element.55), channel_id=1, source_target_pairs={{0,8},{1,2},{2,1},{3,11},{4,12},{5,6},{6,5},{7,15},{8,0},{9,10},{1... | collective-permute-start | bytes 12296 | tf_op jit(solution)/shard_map/ppermute | solution.py:116
  29.9 7.4 %collective-permute-start.16 = (f32[1,32,128]{2,1,0:T(8,128)S(1)}, f32[1,32,128]{2,1,0:T(8,128)S(1)}, u32[]{:S(2)}, u32[]{:S(2)}) collective-permute-start(f32[1,32,128]{2,1,0:T(8,128)S(1)} %get-tuple-element.67), channel_id=1, source_target_pairs={{0,8},{1,9},{2,10},{3,11},{4,12},{5,13},{6,14},{7,15},{8,0},{9,1},... | collective-permute-start | bytes 49160 | tf_op jit(solution)/shard_map/ppermute | solution.py:116
  30.5 6.8 %collective-permute-start.17 = (f32[1,32,128]{2,1,0:T(8,128)S(1)}, f32[1,32,128]{2,1,0:T(8,128)S(1)}, u32[]{:S(2)}, u32[]{:S(2)}) collective-permute-start(f32[1,32,128]{2,1,0:T(8,128)S(1)} %get-tuple-element.68), channel_id=1, source_target_pairs={{0,24},{1,25},{2,26},{3,27},{4,28},{5,29},{6,30},{7,31},{8,16},{9,... | collective-permute-start | bytes 49160 | tf_op jit(solution)/shard_map/ppermute | solution.py:116
  31.7 5.6 %collective-permute-start.18 = (f32[1,16,128]{2,1,0:T(8,128)S(1)}, f32[1,16,128]{2,1,0:T(8,128)S(1)}, u32[]{:S(2)}, u32[]{:S(2)}) collective-permute-start(f32[1,16,128]{2,1,0:T(8,128)S(1)} %get-tuple-element.69), channel_id=1, source_target_pairs={{0,4},{1,5},{2,6},{3,7},{4,0},{5,1},{6,2},{7,3},{8,12},{9,13},{10,... | collective-permute-start | bytes 24584 | tf_op jit(solution)/shard_map/ppermute | solution.py:116
  32.3 5.1 %collective-permute-start.19 = (f32[1,512]{1,0:T(1,128)S(1)}, f32[1,512]{1,0:T(1,128)S(1)}, u32[]{:S(2)}, u32[]{:S(2)}) collective-permute-start(f32[1,512]{1,0:T(1,128)S(1)} %get-tuple-element.70), channel_id=1, source_target_pairs={{0,1},{1,0},{2,3},{3,2},{4,5},{5,4},{6,7},{7,6},{8,9},{9,8},{10,11... | collective-permute-start | bytes 6152 | tf_op jit(solution)/shard_map/ppermute | solution.py:116
  35.8 1.6 %collective-permute-start.20 = (f32[1,512]{1,0:T(1,128)S(1)}, f32[1,512]{1,0:T(1,128)S(1)}, u32[]{:S(2)}, u32[]{:S(2)}) collective-permute-start(f32[1,512]{1,0:T(1,128)S(1)} %get-tuple-element.71), channel_id=1, source_target_pairs={{0,8},{1,2},{2,1},{3,11},{4,12},{5,6},{6,5},{7,15},{8,0},{9,10},{1... | collective-permute-start | bytes 6152 | tf_op jit(solution)/shard_map/ppermute | solution.py:116

commit v2 on v1

--- a/solution.py
+++ b/solution.py
@@ -17,7 +17,7 @@
 HIGH = lax.Precision.HIGHEST
 
 
-def call(body, out_shape, *args, scratch=(), hbm=0):
+def call(body, out_shape, *args, scratch=(), hbm=0, hbm_out=False):
     vmem = pl.BlockSpec(memory_space=pltpu.VMEM)
     args = [pltpu.with_memory_space_constraint(x, pltpu.HBM) for x in args[:hbm]] + list(args[hbm:])
     return pl.pallas_call(
@@ -25,6 +25,7 @@
         out_shape=out_shape,
         in_specs=[pl.BlockSpec(memory_space=pltpu.HBM)] * hbm + [vmem] * (len(args) - hbm),
         scratch_shapes=scratch,
+        **({"out_specs": jax.tree.map(lambda _: pl.BlockSpec(memory_space=pltpu.HBM), out_shape)} if hbm_out else {}),
         compiler_params=pltpu.CompilerParams(vmem_limit_bytes=48 << 20),
     )(*args)
 
@@ -70,7 +71,8 @@
     slots = {k: swap(x, k) for k, x in direct.items()}
     slots[low] = swap(own, low)
     for k in direct:
-        slots[k | low] = swap(slots[k], low)
+        if k | low not in direct:
+            slots[k | low] = swap(slots[k], low)
     return slots
 
 
@@ -216,12 +218,10 @@
             copy.start()
         return copies
 
-    def inner_of(a_ref, h, ready=None):
+    def inner_of(a_ref, h):
         h = h.astype(BF16)
         rows = []
         for b in range(0, nb, group):
-            if ready:
-                ready(b // group)
             both = dot(h[b : b + group, :], a_ref[b : b + group].reshape(group * tri, tri), 1, 1)
             rows += [both[i : i + 1, i * tri : (i + 1) * tri] for i in range(group)]
         return jnp.concatenate(rows, axis=0)
@@ -243,7 +243,7 @@
         pieces += list(zip(hbm[6:], rock))
         copies = load([(src, dst, sems.at[i]) for i, (src, dst) in enumerate(pieces)])
         send_ref[3 * nb :, :] = jnp.zeros((small, tri), F32)
-        for copy in copies[:5]:
+        for copy in copies[: 5 + chunks]:
             copy.wait()
         perm = perm_ref[...]
         send_ref[3 * nb : 3 * nb + links, :nb] = ids_ref[...].astype(F32)
@@ -252,7 +252,7 @@
         send_ref[2 * nb : 3 * nb, :] = den_ref[...] + dot(rows, jnp.ones((rows.shape[0], tri), F32), 0, 0, HIGH)
         h = h_ref[...]
         send_ref[:nb, :] = h
-        send_ref[nb : 2 * nb, :] = w_ref[...] + inner_of(a_ref, h, lambda i: copies[5 + i].wait())
+        send_ref[nb : 2 * nb, :] = w_ref[...] + inner_of(a_ref, h)
         for copy in copies[5 + chunks :]:
             copy.wait()
 
@@ -348,7 +348,6 @@
         mix_ref, den_ref, w_ref, inner_ref, q1_ref, q2_ref, hv_ref, hot1_ref, hot2_ref, u_ref, t0_ref, c_ref = refs[:12]
         got, rest = refs[12 : 12 + ns], refs[12 + ns :]
         h_ref, f_ref, t_ref, wx_ref, wy_ref, *faces = rest[:-1]
-        pick_ref = rest[-1]
         h = sweep(w_ref, den_ref, mix_ref, inner_ref, get_heads(got))
         h_ref[...] = h
         q = jnp.concatenate([q1_ref[...], q2_ref[...]], axis=0)
@@ -358,12 +357,16 @@
         lane = (hv_ref[...] % nz).astype(jnp.int16)
         at = lax.broadcasted_iota(jnp.int16, (nz, tri), 0)
         none = jnp.zeros((), BF16)
-        for b in range(nb):
-            mine = at == lane[b : b + 1, :]
-            pick_ref[:nz, b * tri : (b + 1) * tri] = jnp.where(mine, hi[b : b + 1, :], none)
-            pick_ref[nz:, b * tri : (b + 1) * tri] = jnp.where(mine, lo[b : b + 1, :], none)
-        half = hot1_ref.shape[1]
-        parts = dot(hot1_ref[...], pick_ref[:, :half], 1, 1) + dot(hot2_ref[...], pick_ref[:, half:], 1, 1)
+        parts = jnp.zeros((rows_n, 2 * nz), F32)
+        for b in range(0, nb, 2):
+            tops, lows = [], []
+            for i in range(b, b + 2):
+                mine = at == lane[i : i + 1, :]
+                tops.append(jnp.where(mine, hi[i : i + 1, :], none))
+                lows.append(jnp.where(mine, lo[i : i + 1, :], none))
+            wide = jnp.concatenate([jnp.concatenate(tops, axis=1), jnp.concatenate(lows, axis=1)], axis=0)
+            hot_ref, o = (hot1_ref, b) if b < nb // 2 else (hot2_ref, b - nb // 2)
+            parts = parts + dot(hot_ref[:, o * tri : (o + 2) * tri], wide, 1, 1)
         f = (parts[:, :nz] + parts[:, nz:]).reshape(shape)
         f_ref[...] = f
         t_ref[...] = u_ref[...] + f
@@ -382,13 +385,28 @@
         v_ref[...] = f_ref[...] + t * keep_ref[...] + gain
 
     def last(h_ref, v_ref, t_ref, wx_ref, wy_ref, wz_ref, *rest):
-        got, (head_ref, o_ref) = rest[:-2], rest[-2:]
-        head_ref[...] = h_ref[...]
+        got, (head_ref, out_ref, o_ref, sems) = rest[:-4], rest[-4:]
+        heads = pltpu.make_async_copy(h_ref, head_ref, sems.at[0])
+        heads.start()
         faces = read_faces(got, specs1, 0)
-        o_ref[...] = v_ref[...] + wz_ref[...] * embed_z(ghosts_of("gz", faces["gz"], (1, rows_n)), shape)
+        z = wz_ref[...] * embed_z(ghosts_of("gz", faces["gz"], (1, rows_n)), shape)
         gx = ghosts_of("gx", faces["gx"], (ny, nz))
         gy = ghosts_of("gy", faces["gy"], (nx, nz))
-        add_sides(o_ref, t_ref, wx_ref, wy_ref, gx, gy)
+        step = nx // 2
+        copies = [heads]
+        for k in range(2):
+            part = slice(k * step, (k + 1) * step)
+            o_ref[part] = v_ref[part] + z[part]
+            if k == 0:
+                o_ref[0] = o_ref[0] + wx_ref[0] * (gx[0] - t_ref[0])
+            else:
+                o_ref[nx - 1] = o_ref[nx - 1] + wx_ref[1] * (gx[1] - t_ref[nx - 1])
+            for i, at in enumerate((0, ny - 1)):
+                o_ref[part, at, :] = o_ref[part, at, :] + wy_ref[i, part] * (gy[i][part] - t_ref[part, at, :])
+            copies.append(pltpu.make_async_copy(o_ref.at[pl.ds(k * step, step)], out_ref.at[pl.ds(k * step, step)], sems.at[k + 1]))
+            copies[-1].start()
+        for copy in copies:
+            copy.wait()
 
     send, w, t, c, hv, liq, tf, a = call(
         pre,
@@ -429,7 +447,7 @@
             *[faces[i] for i in xy],
         )
         ride = dict(zip(rides, sends))
-        slots = meet({k: ride.get(k, h) for k in range(n - 1, 0, -1) if not k & low}, ride[low])
+        slots = meet({k: ride.get(k, h) for k in range(n - 1, 0, -1) if not k & low or k == y_at | low}, ride[low])
         den = send[2 * nb : 3 * nb]
         got = [h] + [slots[k] for k in range(1, n)]
 
@@ -489,7 +507,19 @@
     )
     got = exchange(faces, specs1)
     v = call(middle, slab, t1, f, c, keep)
-    h, out = call(last, (blk, slab), h, v, t1, wx, wy, wz, *got)
+    h, out = call(
+        last,
+        (blk, slab),
+        h,
+        v,
+        t1,
+        wx,
+        wy,
+        wz,
+        *got,
+        scratch=[pltpu.VMEM(shape, F32), pltpu.SemaphoreType.DMA((3,))],
+        hbm_out=True,
+    )
     return (h, out)
 
 

time: 38.4 us -> 38.9 us (1.013)
  starting transfers between devices: 15.9 us -> 17.6 us
  waiting for transfers between devices: 13.1 us -> 11.9 us
    ppermute x14, waiting for transfers between devices: 9.94 us -> 7.57 us  [swap(): return lax.ppermute(x, GROUP, [(i, i ^ k) for i in range(n)])]
    ppermute x14, starting transfers between devices: 8.49 us -> 9.87 us  [swap(): return lax.ppermute(x, GROUP, [(i, i ^ k) for i in range(n)])]
    ppermute x7, waiting for transfers between devices: 3.21 us -> 4.37 us  [exchange(): out.append(lax.ppermute(face, AXES, swap_list(axis, r)))]
where the time goes in v2:
time: 38.9 us; the launch traced here: 38.7 us
  starting transfers between devices  17.6 us (45%)
  waiting for transfers between devices  11.9 us (31%)
  Pallas kernels  8.35 us (21%)
  between operations  0.77 us (2%)
    ppermute x14, starting transfers between devices, swap(): return lax.ppermute(x, GROUP, [(i, i ^ k) for i in range(n)])  9.87 us
    pallas_call x10, Pallas kernels, call(): pl.pallas_call(body, out_shape=out_shape, in_specs=[pl.BlockSpec(memory_s...  8.35 us
    ppermute x7, starting transfers between devices, exchange(): out.append(lax.ppermute(face, AXES, swap_list(axis, r)))  7.78 us
    ppermute x14, waiting for transfers between devices, swap(): return lax.ppermute(x, GROUP, [(i, i ^ k) for i in range(n)])  7.57 us
    ppermute x7, waiting for transfers between devices, exchange(): out.append(lax.ppermute(face, AXES, swap_list(axis, r)))  4.37 us
  transfers between devices with their start and end apart: 21, of which 9 were waited for; matrix products, arithmetic and copies ran while one was open for 0% of the time, Pallas kernels for 8%

profile of v2, /device:TPU:0, one launch (start us, length us, event | category | flops | bytes accessed | tf_op | source)
XLA Modules:
  0.0 38.7 jit_solution(5733940854156966794)
XLA Ops:
  0.6 1.9 %shard_map.122 = (f32[104,128]{1,0:T(8,128)S(1)}, f32[32,128]{1,0:T(8,128)S(1)}, f32[16,32,128]{2,1,0:T(8,128)S(1)}, f32[16,32,128]{2,1,0:T(8,128)S(1)}, s32[32,...) custom-call(s32[4,32]{1,0:T(4,128)} %bitcast.2, ...), custom_call_target="tpu_custom_call" | custom-call | tf_op jit(solution)/shard_map/pallas_call | solution.py:23
  2.5 4.0 %collective-permute-start.4 = (f32[104,128]{1,0:T(8,128)S(1)}, f32[104,128]{1,0:T(8,128)S(1)}, u32[]{:S(2)}, u32[]{:S(2)}) collective-permute-start(f32[104,128]{1,0:T(8,128)S(1)} %get-tuple-element.39.send_ref.rest_0_), channel_id=1, source_target_pairs={{0,20},{4,16},{8,28},{12,24},{16,4},{20,0},{24,12},{28,8},{1,21},{... | collective-permute-start | bytes 159752 | tf_op jit(solution)/shard_map/ppermute | solution.py:66
  6.5 0.5 %collective-permute-start.3 = (f32[104,128]{1,0:T(8,128)S(1)}, f32[104,128]{1,0:T(8,128)S(1)}, u32[]{:S(2)}, u32[]{:S(2)}) collective-permute-start(f32[104,128]{1,0:T(8,128)S(1)} %get-tuple-element.39.send_ref.rest_0_), channel_id=1, source_target_pairs={{0,16},{4,20},{8,24},{12,28},{16,0},{20,4},{24,8},{28,12},{1,17},{... | collective-permute-start | bytes 159752 | tf_op jit(solution)/shard_map/ppermute | solution.py:66
  7.0 0.1 collective-permute-start
  7.2 0.0 collective-permute-start.1
  7.2 1.5 %collective-permute-done.4.rest_5_ = f32[104,128]{1,0:T(8,128)S(1)} collective-permute-done((f32[104,128]{1,0:T(8,128)S(1)}, f32[104,128]{1,0:T(8,128)S(1)}, u32[]{:S(2)}, u32[]{:S(2)}) %collective-permute-start.4) | collective-permute-done | bytes 53280 | tf_op jit(solution)/shard_map/ppermute | solution.py:66
  8.6 0.0 collective-permute-start.6
  8.6 2.0 %collective-permute-done.3.rest_4_ = f32[104,128]{1,0:T(8,128)S(1)} collective-permute-done((f32[104,128]{1,0:T(8,128)S(1)}, f32[104,128]{1,0:T(8,128)S(1)}, u32[]{:S(2)}, u32[]{:S(2)}) %collective-permute-start.3) | collective-permute-done | bytes 53280 | tf_op jit(solution)/shard_map/ppermute | solution.py:66
  10.7 0.0 collective-permute-start.5
  10.7 0.5 %collective-permute-done.rest_1_ = f32[104,128]{1,0:T(8,128)S(1)} collective-permute-done((f32[104,128]{1,0:T(8,128)S(1)}, f32[104,128]{1,0:T(8,128)S(1)}, u32[]{:S(2)}, u32[]{:S(2)}) %collective-permute-start) | collective-permute-done | bytes 53280 | tf_op jit(solution)/shard_map/ppermute | solution.py:66
  11.2 0.0 collective-permute-start.2
  11.2 0.2 shard_map.123
  11.4 0.0 collective-permute-done.1.rest_2_
  11.4 0.0 collective-permute-done.6.rest_7_
  11.4 0.5 %collective-permute-done.5.rest_6_ = f32[104,128]{1,0:T(8,128)S(1)} collective-permute-done((f32[104,128]{1,0:T(8,128)S(1)}, f32[104,128]{1,0:T(8,128)S(1)}, u32[]{:S(2)}, u32[]{:S(2)}) %collective-permute-start.5) | collective-permute-done | bytes 53280 | tf_op jit(solution)/shard_map/ppermute | solution.py:66
  11.9 0.5 %collective-permute-done.2.rest_3_ = f32[104,128]{1,0:T(8,128)S(1)} collective-permute-done((f32[104,128]{1,0:T(8,128)S(1)}, f32[104,128]{1,0:T(8,128)S(1)}, u32[]{:S(2)}, u32[]{:S(2)}) %collective-permute-start.2) | collective-permute-done | bytes 53280 | tf_op jit(solution)/shard_map/ppermute | solution.py:66
  12.4 0.8 %shard_map.124 = (f32[32,128]{1,0:T(8,128)S(1)}, f32[96,128]{1,0:T(8,128)S(1)}, f32[96,128]{1,0:T(8,128)S(1)}, f32[64,128]{1,0:T(8,128)S(1)}) custom-call(f32[32,128]{1,0:T(8,128)S(1)} %get-tuple-element.41.w_ref.refs_2_, bf16[32,128,128]{2,1,0:T(8,128)(2,1)S(1)} %get-tuple-element.42.a_ref, bf16[2,32,256]{2,1,0:T(8,128)(2,1)S(1)} %get-tuple-element.40.mix_ref.refs_0_, ...), custom_call_target="tpu_custom_call" | custom-call | tf_op jit(solution)/shard_map/pallas_call | solution.py:23
  13.2 1.6 %collective-permute-start.12 = (f32[96,128]{1,0:T(8,128)S(1)}, f32[96,128]{1,0:T(8,128)S(1)}, u32[]{:S(2)}, u32[]{:S(2)}) collective-permute-start(f32[96,128]{1,0:T(8,128)S(1)} %get-tuple-element.59), channel_id=1, source_target_pairs={{0,16},{4,20},{8,24},{12,28},{16,0},{20,4},{24,8},{28,12},{1,17},{... | collective-permute-start | bytes 147464 | tf_op jit(solution)/shard_map/ppermute | solution.py:66
  14.8 0.0 collective-permute-start.10
  14.8 2.6 %collective-permute-done.12.refs_16_ = f32[96,128]{1,0:T(8,128)S(1)} collective-permute-done((f32[96,128]{1,0:T(8,128)S(1)}, f32[96,128]{1,0:T(8,128)S(1)}, u32[]{:S(2)}, u32[]{:S(2)}) %collective-permute-start.12) | collective-permute-done | bytes 49184 | tf_op jit(solution)/shard_map/ppermute | solution.py:66
  17.4 0.0 collective-permute-start.14
  17.4 1.5 %collective-permute-start.13 = (f32[32,128]{1,0:T(8,128)S(1)}, f32[32,128]{1,0:T(8,128)S(1)}, u32[]{:S(2)}, u32[]{:S(2)}) collective-permute-start(f32[32,128]{1,0:T(8,128)S(1)} %get-tuple-element.46.h_ref.refs_12_), channel_id=1, source_target_pairs={{0,20},{4,16},{8,28},{12,24},{16,4},{20,0},{24,12},{28,8},{1,21},{... | collective-permute-start | bytes 49160 | tf_op jit(solution)/shard_map/ppermute | solution.py:66
  18.9 1.5 %collective-permute-start.9 = (f32[64,128]{1,0:T(8,128)S(1)}, f32[64,128]{1,0:T(8,128)S(1)}, u32[]{:S(2)}, u32[]{:S(2)}) collective-permute-start(f32[64,128]{1,0:T(8,128)S(1)} %get-tuple-element.57), channel_id=1, source_target_pairs={{0,4},{4,0},{8,12},{12,8},{16,20},{20,16},{24,28},{28,24},{1,5},{5... | collective-permute-start | bytes 98312 | tf_op jit(solution)/shard_map/ppermute | solution.py:66
  20.4 1.6 %collective-permute-start.7 = (f32[2,512]{1,0:T(2,128)S(1)}, f32[2,512]{1,0:T(2,128)S(1)}, u32[]{:S(2)}, u32[]{:S(2)}) collective-permute-start(f32[2,512]{1,0:T(2,128)S(1)} %get-tuple-element.54), channel_id=1, source_target_pairs={{0,1},{1,0},{2,3},{3,2},{4,5},{5,4},{6,7},{7,6},{8,9},{9,8},{10,11... | collective-permute-start | bytes 12296 | tf_op jit(solution)/shard_map/ppermute | solution.py:118
  22.0 2.0 %collective-permute-done.7.rest_0_ = f32[2,512]{1,0:T(2,128)S(1)} collective-permute-done((f32[2,512]{1,0:T(2,128)S(1)}, f32[2,512]{1,0:T(2,128)S(1)}, u32[]{:S(2)}, u32[]{:S(2)}) %collective-permute-start.7) | collective-permute-done | bytes 4128 | tf_op jit(solution)/shard_map/ppermute | solution.py:118
  24.0 0.0 collective-permute-start.8
  24.0 1.2 %collective-permute-done.8.rest_1_ = f32[2,512]{1,0:T(2,128)S(1)} collective-permute-done((f32[2,512]{1,0:T(2,128)S(1)}, f32[2,512]{1,0:T(2,128)S(1)}, u32[]{:S(2)}, u32[]{:S(2)}) %collective-permute-start.8) | collective-permute-done | bytes 4128 | tf_op jit(solution)/shard_map/ppermute | solution.py:118
  25.2 0.3 collective-permute-start.11
  25.5 0.0 collective-permute-done.13.refs_17_
  25.5 0.3 collective-permute-start.15
  25.8 0.8 %shard_map.127 = (f32[16,128]{1,0:T(8,128)S(1)}, bf16[512,2048]{1,0:T(8,128)(2,1)S(1)}) custom-call(f32[16,32,128]{2,1,0:T(8,128)S(1)} %get-tuple-element.37.t_ref.refs_10_, s32[32,128]{1,0:T(8,128)S(1)} %get-tuple-element.47.hv_ref.refs_6_, f32[32,128]{1,0:T(8,128)S(1)} %get-tuple-element.48.liq_ref, f32[32,128]{1,0:T(8,128)S(1)} %get-tuple-element.49.tf_ref), custom_call_target="tpu_custom_call" | custom-call | tf_op jit(solution)/shard_map/pallas_call | solution.py:23
  26.6 0.8 %shard_map.126 = (f32[16,128]{1,0:T(8,128)S(1)}, bf16[512,2048]{1,0:T(8,128)(2,1)S(1)}) custom-call(f32[16,32,128]{2,1,0:T(8,128)S(1)} %get-tuple-element.37.t_ref.refs_10_, s32[32,128]{1,0:T(8,128)S(1)} %get-tuple-element.47.hv_ref.refs_6_, f32[32,128]{1,0:T(8,128)S(1)} %get-tuple-element.48.liq_ref, f32[32,128]{1,0:T(8,128)S(1)} %get-tuple-element.49.tf_ref), custom_call_target="tpu_custom_call" | custom-call | tf_op jit(solution)/shard_map/pallas_call | solution.py:23
  27.4 0.6 %shard_map.128 = (f32[16,32,128]{2,1,0:T(8,128)S(1)}, f32[16,32,128]{2,1,0:T(8,128)S(1)}, f32[16,32,128]{2,1,0:T(8,128)S(1)}) custom-call(f32[16,32,128]{2,1,0:T(8,128)S(1)} %get-tuple-element.37.t_ref.refs_10_, f32[16,32,128]{2,1,0:T(8,128)S(1)} %get-tuple-element.38.c_ref.refs_11_, f32[2,512]{1,0:T(2,128)S(1)} %collective-permute-done.7.rest_0_, ...), custom_call_target="tpu_custom_call" | custom-call | tf_op jit(solution)/shard_map/pallas_call | solution.py:23
  28.0 0.4 shard_map.125.refs_3_
  28.4 0.0 collective-permute-done.11.refs_15_
  28.4 0.0 collective-permute-done.15.refs_19_
  28.4 0.0 collective-permute-done.9.refs_13_
  28.4 0.0 collective-permute-done.10.refs_14_
  28.4 0.0 collective-permute-done.14.refs_18_
  28.4 1.6 %shard_map.129 = (f32[32,128]{1,0:T(8,128)S(1)}, f32[16,32,128]{2,1,0:T(8,128)S(1)}, f32[16,32,128]{2,1,0:T(8,128)S(1)}, f32[2,32,128]{2,1,0:T(8,128)S(1)}, f32[...) custom-call(bf16[2,32,256]{2,1,0:T(8,128)(2,1)S(1)} %get-tuple-eleme, ...), custom_call_target="tpu_custom_call" | custom-call | tf_op jit(solution)/shard_map/pallas_call | solution.py:23
  30.0 0.2 collective-permute-start.16
  30.3 0.4 collective-permute-start.17
  30.7 1.6 %collective-permute-start.18 = (f32[1,16,128]{2,1,0:T(8,128)S(1)}, f32[1,16,128]{2,1,0:T(8,128)S(1)}, u32[]{:S(2)}, u32[]{:S(2)}) collective-permute-start(f32[1,16,128]{2,1,0:T(8,128)S(1)} %get-tuple-element.69), channel_id=1, source_target_pairs={{0,4},{1,5},{2,6},{3,7},{4,0},{5,1},{6,2},{7,3},{8,12},{9,13},{10,... | collective-permute-start | bytes 24584 | tf_op jit(solution)/shard_map/ppermute | solution.py:118
  32.2 4.0 %collective-permute-start.19 = (f32[1,512]{1,0:T(1,128)S(1)}, f32[1,512]{1,0:T(1,128)S(1)}, u32[]{:S(2)}, u32[]{:S(2)}) collective-permute-start(f32[1,512]{1,0:T(1,128)S(1)} %get-tuple-element.70), channel_id=1, source_target_pairs={{0,1},{1,0},{2,3},{3,2},{4,5},{5,4},{6,7},{7,6},{8,9},{9,8},{10,11... | collective-permute-start | bytes 6152 | tf_op jit(solution)/shard_map/ppermute | solution.py:118
  36.2 0.0 collective-permute-start.20
  36.2 0.4 %shard_map.130.v_ref = f32[16,32,128]{2,1,0:T(8,128)S(1)} custom-call(f32[16,32,128]{2,1,0:T(8,128)S(1)} %get-tuple-element.61.t_ref, f32[16,32,128]{2,1,0:T(8,128)S(1)} %get-tuple-element.62.f_ref, f32[16,32,128]{2,1,0:T(8,128)S(1)} %get-tuple-element.38.c_ref.refs_11_, f32[16,32,128]{2,1,0:T(8,128)S(1)} %get-tuple-element.63.keep_ref), custom_call_target="tpu_custom_call" | custom-call | tf_op jit(solution)/shard_map/pallas_call | solution.py:23
  36.6 1.2 %collective-permute-done.19.rest_3_ = f32[1,512]{1,0:T(1,128)S(1)} collective-permute-done((f32[1,512]{1,0:T(1,128)S(1)}, f32[1,512]{1,0:T(1,128)S(1)}, u32[]{:S(2)}, u32[]{:S(2)}) %collective-permute-start.19) | collective-permute-done | bytes 2080 | tf_op jit(solution)/shard_map/ppermute | solution.py:118
  37.8 0.0 collective-permute-done.20.rest_4_
  37.8 0.0 collective-permute-done.18.rest_2_
  37.8 0.0 collective-permute-done.16.rest_0_
  37.8 0.0 collective-permute-done.17.rest_1_
  37.8 0.9 %shard_map.131 = (f32[32,128]{1,0:T(8,128)}, f32[16,32,128]{2,1,0:T(8,128)}) custom-call(f32[32,128]{1,0:T(8,128)S(1)} %get-tuple-element.60.h_ref, f32[16,32,128]{2,1,0:T(8,128)S(1)} %shard_map.130.v_ref, f32[16,32,128]{2,1,0:T(8,128)S(1)} %get-tuple-element.61.t_ref, f32[2,32,128]{2,1,0:T(8,128)S(1)} %get-tuple-element.64.wx_ref, ...), custom_call_target="tpu_custom_call" | custom-call | tf_op jit(solution)/shard_map/pallas_call | solution.py:23
  (1 shorter events, 0.0 us)
Async XLA Ops:
  2.5 6.1 %collective-permute-start.4 = (f32[104,128]{1,0:T(8,128)S(1)}, f32[104,128]{1,0:T(8,128)S(1)}, u32[]{:S(2)}, u32[]{:S(2)}) collective-permute-start(f32[104,128]{1,0:T(8,128)S(1)} %get-tuple-element.39.send_ref.rest_0_), channel_id=1, source_target_pairs={{0,20},{4,16},{8,28},{12,24},{16,4},{20,0},{24,12},{28,8},{1,21},{... | collective-permute-start | bytes 159752 | tf_op jit(solution)/shard_map/ppermute | solution.py:66
  6.5 4.1 %collective-permute-start.3 = (f32[104,128]{1,0:T(8,128)S(1)}, f32[104,128]{1,0:T(8,128)S(1)}, u32[]{:S(2)}, u32[]{:S(2)}) collective-permute-start(f32[104,128]{1,0:T(8,128)S(1)} %get-tuple-element.39.send_ref.rest_0_), channel_id=1, source_target_pairs={{0,16},{4,20},{8,24},{12,28},{16,0},{20,4},{24,8},{28,12},{1,17},{... | collective-permute-start | bytes 159752 | tf_op jit(solution)/shard_map/ppermute | solution.py:66
  7.0 4.1 %collective-permute-start = (f32[104,128]{1,0:T(8,128)S(1)}, f32[104,128]{1,0:T(8,128)S(1)}, u32[]{:S(2)}, u32[]{:S(2)}) collective-permute-start(f32[104,128]{1,0:T(8,128)S(1)} %get-tuple-element.39.send_ref.rest_0_), channel_id=1, source_target_pairs={{0,4},{4,0},{8,12},{12,8},{16,20},{20,16},{24,28},{28,24},{1,5},{5... | collective-permute-start | bytes 159752 | tf_op jit(solution)/shard_map/ppermute | solution.py:66
  7.2 4.2 %collective-permute-start.1 = (f32[104,128]{1,0:T(8,128)S(1)}, f32[104,128]{1,0:T(8,128)S(1)}, u32[]{:S(2)}, u32[]{:S(2)}) collective-permute-start(f32[104,128]{1,0:T(8,128)S(1)} %get-tuple-element.39.send_ref.rest_0_), channel_id=1, source_target_pairs={{0,8},{4,12},{8,0},{12,4},{16,24},{20,28},{24,16},{28,20},{1,9},{5... | collective-permute-start | bytes 159752 | tf_op jit(solution)/shard_map/ppermute | solution.py:66
  8.6 2.8 %collective-permute-start.6 = (f32[104,128]{1,0:T(8,128)S(1)}, f32[104,128]{1,0:T(8,128)S(1)}, u32[]{:S(2)}, u32[]{:S(2)}) collective-permute-start(f32[104,128]{1,0:T(8,128)S(1)} %collective-permute-done.4.rest_5_), channel_id=1, source_target_pairs={{0,8},{4,12},{8,0},{12,4},{16,24},{20,28},{24,16},{28,20},{1,9},{5... | collective-permute-start | bytes 159752 | tf_op jit(solution)/shard_map/ppermute | solution.py:66
  10.7 1.2 %collective-permute-start.5 = (f32[104,128]{1,0:T(8,128)S(1)}, f32[104,128]{1,0:T(8,128)S(1)}, u32[]{:S(2)}, u32[]{:S(2)}) collective-permute-start(f32[104,128]{1,0:T(8,128)S(1)} %collective-permute-done.3.rest_4_), channel_id=1, source_target_pairs={{0,8},{4,12},{8,0},{12,4},{16,24},{20,28},{24,16},{28,20},{1,9},{5... | collective-permute-start | bytes 159752 | tf_op jit(solution)/shard_map/ppermute | solution.py:66
  11.2 1.2 %collective-permute-start.2 = (f32[104,128]{1,0:T(8,128)S(1)}, f32[104,128]{1,0:T(8,128)S(1)}, u32[]{:S(2)}, u32[]{:S(2)}) collective-permute-start(f32[104,128]{1,0:T(8,128)S(1)} %collective-permute-done.rest_1_), channel_id=1, source_target_pairs={{0,8},{4,12},{8,0},{12,4},{16,24},{20,28},{24,16},{28,20},{1,9},{5... | collective-permute-start | bytes 159752 | tf_op jit(solution)/shard_map/ppermute | solution.py:66
  13.2 4.2 %collective-permute-start.12 = (f32[96,128]{1,0:T(8,128)S(1)}, f32[96,128]{1,0:T(8,128)S(1)}, u32[]{:S(2)}, u32[]{:S(2)}) collective-permute-start(f32[96,128]{1,0:T(8,128)S(1)} %get-tuple-element.59), channel_id=1, source_target_pairs={{0,16},{4,20},{8,24},{12,28},{16,0},{20,4},{24,8},{28,12},{1,17},{... | collective-permute-start | bytes 147464 | tf_op jit(solution)/shard_map/ppermute | solution.py:66
  14.8 13.6 %collective-permute-start.10 = (f32[96,128]{1,0:T(8,128)S(1)}, f32[96,128]{1,0:T(8,128)S(1)}, u32[]{:S(2)}, u32[]{:S(2)}) collective-permute-start(f32[96,128]{1,0:T(8,128)S(1)} %get-tuple-element.58), channel_id=1, source_target_pairs={{0,8},{4,12},{8,0},{12,4},{16,24},{20,28},{24,16},{28,20},{1,9},{5... | collective-permute-start | bytes 147464 | tf_op jit(solution)/shard_map/ppermute | solution.py:66
  17.4 11.0 %collective-permute-start.14 = (f32[96,128]{1,0:T(8,128)S(1)}, f32[96,128]{1,0:T(8,128)S(1)}, u32[]{:S(2)}, u32[]{:S(2)}) collective-permute-start(f32[96,128]{1,0:T(8,128)S(1)} %collective-permute-done.12.refs_16_), channel_id=1, source_target_pairs={{0,8},{4,12},{8,0},{12,4},{16,24},{20,28},{24,16},{28,20},{1,9},{5... | collective-permute-start | bytes 147464 | tf_op jit(solution)/shard_map/ppermute | solution.py:66
  17.4 8.1 %collective-permute-start.13 = (f32[32,128]{1,0:T(8,128)S(1)}, f32[32,128]{1,0:T(8,128)S(1)}, u32[]{:S(2)}, u32[]{:S(2)}) collective-permute-start(f32[32,128]{1,0:T(8,128)S(1)} %get-tuple-element.46.h_ref.refs_12_), channel_id=1, source_target_pairs={{0,20},{4,16},{8,28},{12,24},{16,4},{20,0},{24,12},{28,8},{1,21},{... | collective-permute-start | bytes 49160 | tf_op jit(solution)/shard_map/ppermute | solution.py:66
  18.9 9.5 %collective-permute-start.9 = (f32[64,128]{1,0:T(8,128)S(1)}, f32[64,128]{1,0:T(8,128)S(1)}, u32[]{:S(2)}, u32[]{:S(2)}) collective-permute-start(f32[64,128]{1,0:T(8,128)S(1)} %get-tuple-element.57), channel_id=1, source_target_pairs={{0,4},{4,0},{8,12},{12,8},{16,20},{20,16},{24,28},{28,24},{1,5},{5... | collective-permute-start | bytes 98312 | tf_op jit(solution)/shard_map/ppermute | solution.py:66
  20.4 3.6 %collective-permute-start.7 = (f32[2,512]{1,0:T(2,128)S(1)}, f32[2,512]{1,0:T(2,128)S(1)}, u32[]{:S(2)}, u32[]{:S(2)}) collective-permute-start(f32[2,512]{1,0:T(2,128)S(1)} %get-tuple-element.54), channel_id=1, source_target_pairs={{0,1},{1,0},{2,3},{3,2},{4,5},{5,4},{6,7},{7,6},{8,9},{9,8},{10,11... | collective-permute-start | bytes 12296 | tf_op jit(solution)/shard_map/ppermute | solution.py:118
  24.0 1.2 %collective-permute-start.8 = (f32[2,512]{1,0:T(2,128)S(1)}, f32[2,512]{1,0:T(2,128)S(1)}, u32[]{:S(2)}, u32[]{:S(2)}) collective-permute-start(f32[2,512]{1,0:T(2,128)S(1)} %get-tuple-element.55), channel_id=1, source_target_pairs={{0,8},{1,2},{2,1},{3,11},{4,12},{5,6},{6,5},{7,15},{8,0},{9,10},{1... | collective-permute-start | bytes 12296 | tf_op jit(solution)/shard_map/ppermute | solution.py:118
  25.2 3.2 %collective-permute-start.11 = (f32[32,128]{1,0:T(8,128)S(1)}, f32[32,128]{1,0:T(8,128)S(1)}, u32[]{:S(2)}, u32[]{:S(2)}) collective-permute-start(f32[32,128]{1,0:T(8,128)S(1)} %get-tuple-element.46.h_ref.refs_12_), channel_id=1, source_target_pairs={{0,12},{4,8},{8,4},{12,0},{16,28},{20,24},{24,20},{28,16},{1,13},{... | collective-permute-start | bytes 49160 | tf_op jit(solution)/shard_map/ppermute | solution.py:66
  25.5 2.9 %collective-permute-start.15 = (f32[32,128]{1,0:T(8,128)S(1)}, f32[32,128]{1,0:T(8,128)S(1)}, u32[]{:S(2)}, u32[]{:S(2)}) collective-permute-start(f32[32,128]{1,0:T(8,128)S(1)} %collective-permute-done.13.refs_17_), channel_id=1, source_target_pairs={{0,8},{4,12},{8,0},{12,4},{16,24},{20,28},{24,16},{28,20},{1,9},{5... | collective-permute-start | bytes 49160 | tf_op jit(solution)/shard_map/ppermute | solution.py:66
  30.0 7.8 %collective-permute-start.16 = (f32[1,32,128]{2,1,0:T(8,128)S(1)}, f32[1,32,128]{2,1,0:T(8,128)S(1)}, u32[]{:S(2)}, u32[]{:S(2)}) collective-permute-start(f32[1,32,128]{2,1,0:T(8,128)S(1)} %get-tuple-element.67), channel_id=1, source_target_pairs={{0,8},{1,9},{2,10},{3,11},{4,12},{5,13},{6,14},{7,15},{8,0},{9,1},... | collective-permute-start | bytes 49160 | tf_op jit(solution)/shard_map/ppermute | solution.py:118
  30.3 7.5 %collective-permute-start.17 = (f32[1,32,128]{2,1,0:T(8,128)S(1)}, f32[1,32,128]{2,1,0:T(8,128)S(1)}, u32[]{:S(2)}, u32[]{:S(2)}) collective-permute-start(f32[1,32,128]{2,1,0:T(8,128)S(1)} %get-tuple-element.68), channel_id=1, source_target_pairs={{0,24},{1,25},{2,26},{3,27},{4,28},{5,29},{6,30},{7,31},{8,16},{9,... | collective-permute-start | bytes 49160 | tf_op jit(solution)/shard_map/ppermute | solution.py:118
  30.7 7.2 %collective-permute-start.18 = (f32[1,16,128]{2,1,0:T(8,128)S(1)}, f32[1,16,128]{2,1,0:T(8,128)S(1)}, u32[]{:S(2)}, u32[]{:S(2)}) collective-permute-start(f32[1,16,128]{2,1,0:T(8,128)S(1)} %get-tuple-element.69), channel_id=1, source_target_pairs={{0,4},{1,5},{2,6},{3,7},{4,0},{5,1},{6,2},{7,3},{8,12},{9,13},{10,... | collective-permute-start | bytes 24584 | tf_op jit(solution)/shard_map/ppermute | solution.py:118
  32.2 5.6 %collective-permute-start.19 = (f32[1,512]{1,0:T(1,128)S(1)}, f32[1,512]{1,0:T(1,128)S(1)}, u32[]{:S(2)}, u32[]{:S(2)}) collective-permute-start(f32[1,512]{1,0:T(1,128)S(1)} %get-tuple-element.70), channel_id=1, source_target_pairs={{0,1},{1,0},{2,3},{3,2},{4,5},{5,4},{6,7},{7,6},{8,9},{9,8},{10,11... | collective-permute-start | bytes 6152 | tf_op jit(solution)/shard_map/ppermute | solution.py:118
  36.2 1.6 %collective-permute-start.20 = (f32[1,512]{1,0:T(1,128)S(1)}, f32[1,512]{1,0:T(1,128)S(1)}, u32[]{:S(2)}, u32[]{:S(2)}) collective-permute-start(f32[1,512]{1,0:T(1,128)S(1)} %get-tuple-element.71), channel_id=1, source_target_pairs={{0,8},{1,2},{2,1},{3,11},{4,12},{5,6},{6,5},{7,15},{8,0},{9,10},{1... | collective-permute-start | bytes 6152 | tf_op jit(solution)/shard_map/ppermute | solution.py:118
